TPU v7x, 768 devices: a whole 4x8x12 slice. The times are simulated.
768 devices in a mesh: dp: 48 (over z_lo, x, core), grp: 16 (over y, z_hi).
Axes of the slice: x: 4, y: 8, z: 12 (z_hi: 2, z_lo: 6; z = z_hi * 6 + z_lo), core: 2. Of those that a mesh axis runs over, the one named last changes fastest.
Arguments:
- embeddings: bfloat16 [294912, 512], P(('dp', 'grp')), may hold values from -0.31 to 0.31
- order: int32 [768, 384], P(('dp', 'grp')), may hold values from 0 to 383, as said below
Outputs:
- emb_grad: bfloat16 [294912, 512], P(('dp', 'grp'))
- row_loss: float32 [768, 384], P(('dp', 'grp'))
Inputs may be any that keep to these rules, and one draw needn't show every extreme that they name: Each row of order is a permutation of 0 .. 383.
All inputs are finite; a program needn't handle non-finite values.
Results may differ from a plain program's by a relative error of at most 0.0046.
Values may be sent and summed in bfloat16 or wider, within the bound.
No kernel may reach another device: no remote copies, remote signals or barrier semaphores. Data moves between devices by JAX's collectives and lax.ppermute only.
A program may use at most 32 MiB of HBM per device.

v0:
```python
import jax
import jax.numpy as jnp
from jax import lax
from jax.experimental import pallas as pl
from jax.experimental.pallas import tpu as pltpu
from jax.sharding import Mesh
from jax.sharding import PartitionSpec as P


K = 16
gamma = 16.0
F32 = jnp.float32
BF16 = jnp.bfloat16
WHERE = ("zl", "x", "zh")
LIMIT = 20 * 2**20


def rows_by_rows(a, b):
    return lax.dot_general(a, b, (((1,), (1,)), ((), ())), preferred_element_type=F32)


def block_ids(rows, core, shape, axis):
    half = rows // 2
    i = lax.broadcasted_iota(jnp.int32, shape, axis)
    source = jnp.where(i < half, core, 1 - core)
    i = jnp.where(i < half, i, i - half)
    return (i // 8) * 16 + source * 8 + i % 8


def chip_rows(own, sib):
    half = own.shape[0] // 2
    return jnp.concatenate([own[0:half], sib[0:half], own[half:], sib[half:]], axis=0)


def as_row(column):
    return jnp.broadcast_to(column, (column.shape[0], 128)).T[0:1]


def mask_kernel(core_ref, oa_ref, ob_ref, sign_ref):
    core = core_ref[0]

    @pl.when(core == 0)
    def _():
        rows = oa_ref.shape[1]
        ids = block_ids(rows, core, (rows, rows), 0)
        slot = lax.broadcasted_iota(jnp.int32, (rows, 128), 0) // K
        kind = lax.broadcasted_iota(jnp.int32, (rows, 128), 1)
        hot = []
        for which, ref in enumerate((oa_ref, ob_ref)):
            chosen = jnp.where(ids == ref[...], 1.0, 0.0).astype(BF16)
            table = jnp.where(kind == slot + which * (rows // K), 1.0, 0.0).astype(BF16)
            hot.append(jnp.dot(chosen, table, preferred_element_type=F32).astype(BF16))
        hot = jnp.concatenate(hot, axis=0)
        same = rows_by_rows(hot, hot)
        shape = (2 * rows, 2 * rows)
        diagonal = lax.broadcasted_iota(jnp.int32, shape, 0) == lax.broadcasted_iota(
            jnp.int32, shape, 1
        )
        sign_ref[...] = jnp.where(diagonal, 0.0, 1.0 - 2.0 * same)


def pack_kernel(core_ref, x_ref, oa_ref, ob_ref, full_ref, one_ref, two_ref):
    core = core_ref[0]
    half = one_ref.shape[0]
    for which in range(2):
        x = x_ref[:, which].astype(F32).reshape(half, x_ref.shape[-1])
        inv = lax.rsqrt(jnp.sum(x * x, axis=1, keepdims=True) + 1e-06)
        unit = (x * inv).astype(BF16)
        full_ref[which * half : (which + 1) * half] = unit

        @pl.when(core == 1 - which)
        def _():
            one_ref[...] = unit

        @pl.when(core == which)
        def _():
            two_ref[...] = unit


def near_kernel(core_ref, own_ref, sib_ref, n1_ref, n2_ref, e_ref, sums_ref):
    core = core_ref[0]
    rows = own_ref.shape[0]
    chip = chip_rows(own_ref[...], sib_ref[...])
    near = chip_rows(n2_ref[...], n1_ref[...])
    for b in range(2):
        e = jnp.exp(gamma * rows_by_rows(chip[b * rows : (b + 1) * rows], near))
        e_ref[b * rows : (b + 1) * rows] = e

        @pl.when(core == 0)
        def _():
            sums_ref[b * rows : (b + 1) * rows, 0:1] = jnp.sum(e, axis=1, keepdims=True)


def own_kernel(core_ref, own_ref, sib_ref, sign_ref, d_ref, sums_ref):
    @pl.when(core_ref[0] == 0)
    def _():
        rows = own_ref.shape[0]
        chip = chip_rows(own_ref[...], sib_ref[...])
        for b in range(2):
            part = slice(b * rows, (b + 1) * rows)
            sign = sign_ref[part]
            d = jnp.exp(gamma * sign * rows_by_rows(chip[part], chip))
            d_ref[part] = d
            mine = sign[:, b * rows : (b + 1) * rows]
            here = d[:, b * rows : (b + 1) * rows]
            pos = jnp.where(mine < 0.0, here, 0.0)
            neg = jnp.where(mine > 0.0, here, 0.0)
            total = jnp.sum(neg, axis=1, keepdims=True)
            if b == 1:
                total = total + jnp.sum(d[:, 0:rows], axis=1, keepdims=True)
            sums_ref[part, 0:1] = jnp.sum(pos, axis=1, keepdims=True)
            sums_ref[part, 1:2] = total


def far_kernel(
    core_ref, own_ref, sib_ref, q1_ref, q2_ref, near_sums_ref, sums_ref, oa_ref, ob_ref,
    f_ref, cols_ref, lanes_ref, loss_ref,
):
    core = core_ref[0]
    rows = own_ref.shape[0]
    half = rows // 2
    far = jnp.concatenate([q2_ref[...], q1_ref[...]], axis=0)

    @pl.when(core == 1)
    def _():
        block = jnp.concatenate([own_ref[half:], sib_ref[half:]], axis=0)
        f_ref[...] = jnp.exp(gamma * rows_by_rows(block, far))

    @pl.when(core == 0)
    def _():
        block = jnp.concatenate([own_ref[0:half], sib_ref[0:half]], axis=0)
        f = jnp.exp(gamma * rows_by_rows(block, far))
        f_ref[...] = f
        ids = block_ids(rows, core, (rows, rows), 0)
        for b, order in enumerate((oa_ref, ob_ref)):
            part = slice(b * rows, (b + 1) * rows)
            pos_sum = sums_ref[part, 0:1]
            neg_sum = sums_ref[part, 1:2] + near_sums_ref[part, 0:1]
            if b == 0:
                neg_sum = neg_sum + jnp.sum(f, axis=1, keepdims=True)
            product = pos_sum * neg_sum
            weight = product / (1.0 + product)
            on_neg = gamma * weight / neg_sum
            on_pos = gamma * weight / pos_sum
            cols_ref[part, 0:1] = on_neg
            cols_ref[part, 1:2] = on_pos
            lanes_ref[0:1, part] = as_row(on_neg)
            lanes_ref[1:2, part] = as_row(on_pos)
            loss = jnp.log(1.0 + product)
            loss_ref[b : b + 1] = jnp.sum(
                jnp.where(ids == order[...], loss, 0.0), axis=0, keepdims=True
            )


def split_store(b, total, keep_ref, send_ref):
    half = total.shape[0] // 2
    keep_ref[b * half : (b + 1) * half] = total[0:half]
    send_ref[b * half : (b + 1) * half] = total[half:]


def below_kernel(
    core_ref, own_ref, sib_ref, n1_ref, n2_ref, q1_ref, q2_ref,
    e_ref, d_ref, sign_ref, f_ref, cols_ref, lanes_ref, keep_ref, send_ref,
):
    core = core_ref[0]

    @pl.when(core == 0)
    def _():
        rows = own_ref.shape[0]
        chip = chip_rows(own_ref[...], sib_ref[...])
        near = chip_rows(n2_ref[...], n1_ref[...])
        far = jnp.concatenate([q2_ref[...], q1_ref[...]], axis=0)
        zero = jnp.zeros((1, rows), F32)
        for b in range(2):
            part = slice(b * rows, (b + 1) * rows)
            on_neg = cols_ref[part, 0:1]
            on_pos = cols_ref[part, 1:2]
            lanes_neg = lanes_ref[0:1]
            lanes_pos = lanes_ref[1:2]
            d = d_ref[part]
            sign = sign_ref[part]
            columns = []
            for other in range(2):
                there = slice(other * rows, (other + 1) * rows)
                if other == b:
                    here = sign[:, there]
                    up = on_neg + lanes_neg[:, there]
                    down = on_pos + lanes_pos[:, there]
                    scale = jnp.where(here > 0.0, up, jnp.where(here < 0.0, -down, 0.0))
                elif b == 0:
                    scale = lanes_neg[:, there]
                else:
                    scale = on_neg
                columns.append((scale * d[:, there]).astype(BF16))
            total = jnp.dot(jnp.concatenate(columns, axis=1), chip, preferred_element_type=F32)
            total = total + jnp.dot(
                (on_neg * e_ref[part]).astype(BF16), near, preferred_element_type=F32
            )
            if b == 0:
                total = total + jnp.dot(
                    (on_neg * f_ref[...]).astype(BF16), far, preferred_element_type=F32
                )
            split_store(b, total, keep_ref, send_ref)


def above_kernel(
    core_ref, n1_ref, n2_ref, q1_ref, q2_ref, e_ref, f_ref, on_near_ref, on_far_ref, keep_in, send_in,
    keep_ref, send_ref,
):
    core = core_ref[0]

    @pl.when(core == 1)
    def _():
        rows = n1_ref.shape[0]
        near = chip_rows(n2_ref[...], n1_ref[...])
        far = jnp.concatenate([q2_ref[...], q1_ref[...]], axis=0)
        for b in range(2):
            part = slice(b * rows, (b + 1) * rows)
            total = jnp.dot(
                (on_near_ref[...] * e_ref[part]).astype(BF16), near, preferred_element_type=F32
            )
            if b == 1:
                total = total + jnp.dot(
                    (on_far_ref[...] * f_ref[...]).astype(BF16), far, preferred_element_type=F32
                )
            split_store(b, total, keep_ref, send_ref)


def final_kernel(x_ref, keep_ref, other_ref, la_ref, lb_ref, grad_ref, loss_ref):
    loss_ref[...] = la_ref[...] + lb_ref[...]
    features = x_ref.shape[-1]
    half = keep_ref.shape[0] // 2
    for which in range(2):
        part = slice(which * half, (which + 1) * half)
        total = keep_ref[part] + other_ref[part]
        x = x_ref[:, which].astype(F32).reshape(half, features)
        inv = lax.rsqrt(jnp.sum(x * x, axis=1, keepdims=True) + 1e-06)
        u = x * inv
        grad = (total - u * jnp.sum(u * total, axis=1, keepdims=True)) * inv
        grad_ref[:, which] = grad.reshape(half // 8, 8, features).astype(BF16)


VMEM = pl.BlockSpec(memory_space=pltpu.VMEM)
SMEM = pl.BlockSpec(memory_space=pltpu.SMEM)


def shape(*size, dtype=F32):
    return jax.ShapeDtypeStruct(size, dtype)


def call(kernel, inputs, outputs, work, aliases=None):
    return pl.pallas_call(
        kernel,
        out_shape=outputs,
        in_specs=[SMEM if a.ndim == 1 else VMEM for a in inputs],
        out_specs=jax.tree.map(lambda _: VMEM, outputs),
        input_output_aliases=aliases or {},
        compiler_params=pltpu.CompilerParams(vmem_limit_bytes=LIMIT),
        cost_estimate=pl.CostEstimate(
            flops=int(work * 10**9), bytes_accessed=10**5, transcendentals=0
        ),
    )(*inputs)


def on_device(embeddings, order):
    rows, features = embeddings.shape
    peers = lax.axis_size(WHERE)
    per_peer = rows // peers
    half = rows // 2
    core = lax.axis_index("c").astype(jnp.int32).reshape(1)
    ring = lax.axis_size("y")

    def fetch_order(h):
        return lax.ppermute(order, ("c", "zh"), [(c * 2 + h, c) for c in range(2)])

    def send_loss(loss, h):
        return lax.ppermute(loss, ("c", "zh"), [(z, z * 2 + h) for z in range(2)])

    def along(value, moves):
        route = [(a * ring + y, b * ring + (y + s) % ring) for a, b, s in moves for y in range(ring)]
        return lax.ppermute(value, ("c", "y"), route)

    oa, ob = fetch_order(0), fetch_order(1)
    arrived = lax.all_to_all(
        embeddings.reshape(peers, per_peer, features), WHERE, 0, 0, tiled=True
    ).reshape(peers // 2, 2, per_peer, features)
    block = shape(rows, features, dtype=BF16)
    half_block = shape(half, features, dtype=BF16)

    own, one, two = call(
        pack_kernel, (core, arrived, oa, ob), (block, half_block, half_block), 0.01
    )
    n1 = along(own, ((0, 0, 1), (1, 1, -1)))
    n2 = along(own, ((1, 0, 1), (0, 1, -1)))
    q1 = along(one, ((0, 0, 2), (1, 1, -2)))
    q2 = along(two, ((1, 0, 2), (0, 1, -2)))
    sib = along(own, ((0, 1, 0), (1, 0, 0)))

    sign = call(mask_kernel, (core, oa, ob), shape(2 * rows, 2 * rows), 0.5)
    e, near_sums = call(
        near_kernel, (core, own, sib, n1, n2), (shape(2 * rows, 2 * rows), shape(2 * rows, 8)), 0.8
    )
    d, own_sums = call(
        own_kernel, (core, own, sib, sign), (shape(2 * rows, 2 * rows), shape(2 * rows, 8)), 0.8
    )
    f, cols, lanes, loss = call(
        far_kernel,
        (core, own, sib, q1, q2, near_sums, own_sums, oa, ob),
        (shape(rows, rows), shape(2 * rows, 8), shape(2, 2 * rows), shape(2, rows)),
        0.2,
    )
    on_near = along(lanes[0:1], ((0, 1, -1),))
    on_far = along(lanes[0:1, 0:rows], ((0, 1, -2),))
    half_grads = (shape(rows, features), shape(rows, features))
    keep, send = call(
        below_kernel, (core, own, sib, n1, n2, q1, q2, e, d, sign, f, cols, lanes), half_grads, 1.4
    )
    keep, send = call(
        above_kernel,
        (core, n1, n2, q1, q2, e, f, on_near, on_far, keep, send),
        half_grads,
        0.8,
        {9: 0, 10: 1},
    )
    other = along(send, ((0, 1, 0), (1, 0, 0)))
    grad, row_loss = call(
        final_kernel,
        (arrived, keep, other, send_loss(loss[0:1], 0), send_loss(loss[1:2], 1)),
        (shape(peers // 2, 2, per_peer, features, dtype=BF16), shape(1, rows)),
        0.01,
    )
    sent_back = lax.all_to_all(
        grad.reshape(peers, per_peer, features), WHERE, 0, 0, tiled=True
    )
    return sent_back.reshape(rows, features), row_loss


def solution(mesh):
    dp, grp = mesh.devices.shape
    parts = Mesh(
        mesh.devices.reshape(dp // 8, 4, 2, grp // 2, 2), ("zl", "x", "c", "y", "zh")
    )
    placed = P(("zl", "x", "c", "y", "zh"), None)

    def step(embeddings, order):
        return on_device(embeddings, order)

    step = jax.shard_map(
        step, mesh=parts, in_specs=(placed, placed), out_specs=(placed, placed), check_vma=False
    )
    return step
```

profile of v0, /device:TPU:56, one launch (start us, length us, event | category | flops | bytes accessed | tf_op | source)
XLA Modules:
  0.0 117.9 jit_solution(10681967436336747991)
XLA Ops:
  0.6 18.3 %all-to-all-start = ((bf16[48,8,512]{2,1,0:T(8,128)(2,1)}), bf16[48,8,512]{2,1,0:T(8,128)(2,1)S(1)}, u32[]{:S(2)}, u32[]{:S(2)}) async-start(bf16[48,8,512]{2,1,0:T(8,128)(2,1)} %bitcast.9), calls=%async_computation | async-start | bytes 786432 | tf_op jit(solution)/shard_map/all_to_all | solution.py:284
  18.9 1.3 %collective-permute-start.1 = (s32[1,384]{1,0:T(1,128)}, s32[1,384]{1,0:T(1,128)S(1)}, u32[]{:S(2)}, u32[]{:S(2)}) collective-permute-start(s32[1,384]{1,0:T(1,128)} %param.3), channel_id=1, source_target_pairs={{1,0},{17,1},{3,2},{19,3},{5,4},{21,5},{7,6},{23,7},{9,8},{25,9},{... | collective-permute-start | bytes 4616 | tf_op jit(solution)/shard_map/ppermute | solution.py:274
  20.2 1.3 %collective-permute-start = (s32[1,384]{1,0:T(1,128)}, s32[1,384]{1,0:T(1,128)S(1)}, u32[]{:S(2)}, u32[]{:S(2)}) collective-permute-start(s32[1,384]{1,0:T(1,128)} %param.3), channel_id=1, source_target_pairs={{0,0},{16,1},{2,2},{18,3},{4,4},{20,5},{6,6},{22,7},{8,8},{24,9},{... | collective-permute-start | bytes 4616 | tf_op jit(solution)/shard_map/ppermute | solution.py:274
  21.6 18.1 %collective-permute-done.1.ob_ref = s32[1,384]{1,0:T(1,128)S(1)} collective-permute-done((s32[1,384]{1,0:T(1,128)}, s32[1,384]{1,0:T(1,128)S(1)}, u32[]{:S(2)}, u32[]{:S(2)}) %collective-permute-start.1) | collective-permute-done | bytes 1568 | tf_op jit(solution)/shard_map/ppermute | solution.py:274
  39.7 0.0 collective-permute-done.oa_ref
  39.7 1.0 all-to-all-done
  40.7 0.3 shard_map.41
  41.0 1.9 %collective-permute-start.6 = (bf16[384,512]{1,0:T(8,128)(2,1)S(1)}, bf16[384,512]{1,0:T(8,128)(2,1)S(1)}, u32[]{:S(2)}, u32[]{:S(2)}) collective-permute-start(bf16[384,512]{1,0:T(8,128)(2,1)S(1)} %get-tuple-element.19.own_ref), channel_id=1, source_target_pairs={{0,16},{2,18},{4,20},{6,22},{8,24},{10,26},{12,28},{14,30},{16,0},... | collective-permute-start | bytes 1179656 | tf_op jit(solution)/shard_map/ppermute | solution.py:281
  42.9 3.4 %collective-permute-start.3 = (bf16[384,512]{1,0:T(8,128)(2,1)S(1)}, bf16[384,512]{1,0:T(8,128)(2,1)S(1)}, u32[]{:S(2)}, u32[]{:S(2)}) collective-permute-start(bf16[384,512]{1,0:T(8,128)(2,1)S(1)} %get-tuple-element.19.own_ref), channel_id=1, source_target_pairs={{16,2},{18,4},{20,6},{22,8},{24,10},{26,12},{28,14},{30,0},{0,30},... | collective-permute-start | bytes 1179656 | tf_op jit(solution)/shard_map/ppermute | solution.py:281
  46.3 3.8 %collective-permute-start.2 = (bf16[384,512]{1,0:T(8,128)(2,1)S(1)}, bf16[384,512]{1,0:T(8,128)(2,1)S(1)}, u32[]{:S(2)}, u32[]{:S(2)}) collective-permute-start(bf16[384,512]{1,0:T(8,128)(2,1)S(1)} %get-tuple-element.19.own_ref), channel_id=1, source_target_pairs={{0,2},{2,4},{4,6},{6,8},{8,10},{10,12},{12,14},{14,0},{16,30},{18,... | collective-permute-start | bytes 1179656 | tf_op jit(solution)/shard_map/ppermute | solution.py:281
  50.1 1.9 %collective-permute-start.4 = (bf16[192,512]{1,0:T(8,128)(2,1)S(1)}, bf16[192,512]{1,0:T(8,128)(2,1)S(1)}, u32[]{:S(2)}, u32[]{:S(2)}) collective-permute-start(bf16[192,512]{1,0:T(8,128)(2,1)S(1)} %get-tuple-element.20), channel_id=1, source_target_pairs={{0,4},{2,6},{4,8},{6,10},{8,12},{10,14},{12,0},{14,2},{16,28},{18,... | collective-permute-start | bytes 589832 | tf_op jit(solution)/shard_map/ppermute | solution.py:281
  52.0 4.2 %collective-permute-start.5 = (bf16[192,512]{1,0:T(8,128)(2,1)S(1)}, bf16[192,512]{1,0:T(8,128)(2,1)S(1)}, u32[]{:S(2)}, u32[]{:S(2)}) collective-permute-start(bf16[192,512]{1,0:T(8,128)(2,1)S(1)} %get-tuple-element.21), channel_id=1, source_target_pairs={{16,4},{18,6},{20,8},{22,10},{24,12},{26,14},{28,0},{30,2},{0,28},... | collective-permute-start | bytes 589832 | tf_op jit(solution)/shard_map/ppermute | solution.py:281
  56.2 0.7 shard_map.43.sign_ref
  56.9 0.0 collective-permute-done.6.sib_ref
  56.9 1.1 shard_map.44
  58.1 0.0 collective-permute-done.2.n1_ref
  58.1 1.5 %shard_map.42 = (f32[768,768]{1,0:T(8,128)S(1)}, f32[768,8]{1,0:T(8,128)S(1)}) custom-call(s32[1]{0:T(128)} %bitcast.2.core_ref, bf16[384,512]{1,0:T(8,128)(2,1)S(1)} %get-tuple-element.19.own_ref, bf16[384,512]{1,0:T(8,128)(2,1)S(1)} %collective-permute-done.6.sib_ref, bf16[384,512]{1,0:T(8,128)(2,1)S(1)} %collective-permute-done.2.n1_ref, ...), custom_call_target="tpu_custom_call" | custom-call | flops 800000000 | bytes 100000 | tf_op jit(solution)/shard_map/pallas_call | solution.py:252
  59.6 5.1 %collective-permute-done.4.q1_ref = bf16[192,512]{1,0:T(8,128)(2,1)S(1)} collective-permute-done((bf16[192,512]{1,0:T(8,128)(2,1)S(1)}, bf16[192,512]{1,0:T(8,128)(2,1)S(1)}, u32[]{:S(2)}, u32[]{:S(2)}) %collective-permute-start.4) | collective-permute-done | bytes 196640 | tf_op jit(solution)/shard_map/ppermute | solution.py:281
  64.7 0.8 collective-permute-done.5.q2_ref
  65.4 1.5 %shard_map.45 = (f32[384,384]{1,0:T(8,128)S(1)}, f32[768,8]{1,0:T(8,128)S(1)}, f32[2,768]{1,0:T(2,128)S(1)}, f32[2,384]{1,0:T(2,128)S(1)}) custom-call(s32[1]{0:T(128)} %bitcast.2.core_ref, bf16[384,512]{1,0:T(8,128)(2,1)S(1)} %get-tuple-element.19.own_ref, bf16[384,512]{1,0:T(8,128)(2,1)S(1)} %collective-permute-done.6.sib_ref, ...), custom_call_target="tpu_custom_call" | custom-call | flops 200000000 | bytes 100000 | tf_op jit(solution)/shard_map/pallas_call | solution.py:252
  66.9 1.3 %collective-permute-start.8 = (f32[1,384]{1,0:T(1,128)S(1)}, f32[1,384]{1,0:T(1,128)S(1)}, u32[]{:S(2)}, u32[]{:S(2)}) collective-permute-start(f32[1,384]{1,0:T(1,128)S(1)} %slice.13), channel_id=1, source_target_pairs={{0,28},{2,30},{4,16},{6,18},{8,20},{10,22},{12,24},{14,26},{1,29},... | collective-permute-start | bytes 4616 | tf_op jit(solution)/shard_map/ppermute | solution.py:281
  68.2 2.9 %collective-permute-start.7 = (f32[1,768]{1,0:T(1,128)S(1)}, f32[1,768]{1,0:T(1,128)S(1)}, u32[]{:S(2)}, u32[]{:S(2)}) collective-permute-start(f32[1,768]{1,0:T(1,128)S(1)} %slice.12), channel_id=1, source_target_pairs={{0,30},{2,16},{4,18},{6,20},{8,22},{10,24},{12,26},{14,28},{1,31},... | collective-permute-start | bytes 9224 | tf_op jit(solution)/shard_map/ppermute | solution.py:281
  71.1 1.7 %shard_map.46 = (f32[384,512]{1,0:T(8,128)S(1)}, f32[384,512]{1,0:T(8,128)S(1)}) custom-call(s32[1]{0:T(128)} %bitcast.2.core_ref, bf16[384,512]{1,0:T(8,128)(2,1)S(1)} %get-tuple-element.19.own_ref, bf16[384,512]{1,0:T(8,128)(2,1)S(1)} %collective-permute-done.6.sib_ref, bf16[384,512]{1,0:T(8,128)(2,1)S(1)} %collective-permute-done.2.n1_ref, ...), custom_call_target="tpu_custom_call" | custom-call | flops 1400000000 | bytes 100000 | tf_op jit(solution)/shard_map/pallas_call | solution.py:252
  72.8 0.0 collective-permute-done.8.on_far_ref
  72.9 5.1 %collective-permute-start.9 = (f32[384,512]{1,0:T(8,128)S(1)}, f32[384,512]{1,0:T(8,128)S(1)}, u32[]{:S(2)}, u32[]{:S(2)}) collective-permute-start(f32[384,512]{1,0:T(8,128)S(1)} %get-tuple-element.32), channel_id=1, source_target_pairs={{0,16},{2,18},{4,20},{6,22},{8,24},{10,26},{12,28},{14,30},{16,0},... | collective-permute-start | bytes 2359304 | tf_op jit(solution)/shard_map/ppermute | solution.py:281
  78.0 3.8 %collective-permute-start.11 = (f32[1,384]{1,0:T(1,128)S(1)}, f32[1,384]{1,0:T(1,128)S(1)}, u32[]{:S(2)}, u32[]{:S(2)}) collective-permute-start(f32[1,384]{1,0:T(1,128)S(1)} %get-tuple-element.36), channel_id=1, source_target_pairs={{0,1},{1,17},{2,3},{3,19},{4,5},{5,21},{6,7},{7,23},{8,9},{9,25},{... | collective-permute-start | bytes 4616 | tf_op jit(solution)/shard_map/ppermute | solution.py:277
  81.8 0.7 collective-permute-start.10
  82.5 0.6 collective-permute-done.11.lb_ref
  83.1 0.0 collective-permute-done.10.la_ref
  83.1 0.9 shard_map.48
  84.0 33.1 %all_to_all.10 = bf16[48,8,512]{2,1,0:T(8,128)(2,1)S(1)} all-to-all(bf16[48,8,512]{2,1,0:T(8,128)(2,1)S(1)} %bitcast.7), channel_id=1, replica_groups=mesh['zl'=6,'x'=4,'c'=2,'y'=8,'zh'=2] {'zl','x','zh'}, dimensions={0} | all-to-all | bytes 786432 | tf_op jit(solution)/shard_map/all_to_all | solution.py:332
  117.1 0.7 copy.9
  (7 shorter events, 0.0 us)
Async XLA Ops:
  0.6 40.1 %all-to-all-start = ((bf16[48,8,512]{2,1,0:T(8,128)(2,1)}), bf16[48,8,512]{2,1,0:T(8,128)(2,1)S(1)}, u32[]{:S(2)}, u32[]{:S(2)}) async-start(bf16[48,8,512]{2,1,0:T(8,128)(2,1)} %bitcast.9), calls=%async_computation | async-start | bytes 786432 | tf_op jit(solution)/shard_map/all_to_all | solution.py:284
  18.9 20.7 %collective-permute-start.1 = (s32[1,384]{1,0:T(1,128)}, s32[1,384]{1,0:T(1,128)S(1)}, u32[]{:S(2)}, u32[]{:S(2)}) collective-permute-start(s32[1,384]{1,0:T(1,128)} %param.3), channel_id=1, source_target_pairs={{1,0},{17,1},{3,2},{19,3},{5,4},{21,5},{7,6},{23,7},{9,8},{25,9},{... | collective-permute-start | bytes 4616 | tf_op jit(solution)/shard_map/ppermute | solution.py:274
  20.2 19.4 %collective-permute-start = (s32[1,384]{1,0:T(1,128)}, s32[1,384]{1,0:T(1,128)S(1)}, u32[]{:S(2)}, u32[]{:S(2)}) collective-permute-start(s32[1,384]{1,0:T(1,128)} %param.3), channel_id=1, source_target_pairs={{0,0},{16,1},{2,2},{18,3},{4,4},{20,5},{6,6},{22,7},{8,8},{24,9},{... | collective-permute-start | bytes 4616 | tf_op jit(solution)/shard_map/ppermute | solution.py:274
  41.0 15.9 %collective-permute-start.6 = (bf16[384,512]{1,0:T(8,128)(2,1)S(1)}, bf16[384,512]{1,0:T(8,128)(2,1)S(1)}, u32[]{:S(2)}, u32[]{:S(2)}) collective-permute-start(bf16[384,512]{1,0:T(8,128)(2,1)S(1)} %get-tuple-element.19.own_ref), channel_id=1, source_target_pairs={{0,16},{2,18},{4,20},{6,22},{8,24},{10,26},{12,28},{14,30},{16,0},... | collective-permute-start | bytes 1179656 | tf_op jit(solution)/shard_map/ppermute | solution.py:281
  42.9 15.1 %collective-permute-start.3 = (bf16[384,512]{1,0:T(8,128)(2,1)S(1)}, bf16[384,512]{1,0:T(8,128)(2,1)S(1)}, u32[]{:S(2)}, u32[]{:S(2)}) collective-permute-start(bf16[384,512]{1,0:T(8,128)(2,1)S(1)} %get-tuple-element.19.own_ref), channel_id=1, source_target_pairs={{16,2},{18,4},{20,6},{22,8},{24,10},{26,12},{28,14},{30,0},{0,30},... | collective-permute-start | bytes 1179656 | tf_op jit(solution)/shard_map/ppermute | solution.py:281
  46.3 11.8 %collective-permute-start.2 = (bf16[384,512]{1,0:T(8,128)(2,1)S(1)}, bf16[384,512]{1,0:T(8,128)(2,1)S(1)}, u32[]{:S(2)}, u32[]{:S(2)}) collective-permute-start(bf16[384,512]{1,0:T(8,128)(2,1)S(1)} %get-tuple-element.19.own_ref), channel_id=1, source_target_pairs={{0,2},{2,4},{4,6},{6,8},{8,10},{10,12},{12,14},{14,0},{16,30},{18,... | collective-permute-start | bytes 1179656 | tf_op jit(solution)/shard_map/ppermute | solution.py:281
  50.1 14.6 %collective-permute-start.4 = (bf16[192,512]{1,0:T(8,128)(2,1)S(1)}, bf16[192,512]{1,0:T(8,128)(2,1)S(1)}, u32[]{:S(2)}, u32[]{:S(2)}) collective-permute-start(bf16[192,512]{1,0:T(8,128)(2,1)S(1)} %get-tuple-element.20), channel_id=1, source_target_pairs={{0,4},{2,6},{4,8},{6,10},{8,12},{10,14},{12,0},{14,2},{16,28},{18,... | collective-permute-start | bytes 589832 | tf_op jit(solution)/shard_map/ppermute | solution.py:281
  52.0 13.4 %collective-permute-start.5 = (bf16[192,512]{1,0:T(8,128)(2,1)S(1)}, bf16[192,512]{1,0:T(8,128)(2,1)S(1)}, u32[]{:S(2)}, u32[]{:S(2)}) collective-permute-start(bf16[192,512]{1,0:T(8,128)(2,1)S(1)} %get-tuple-element.21), channel_id=1, source_target_pairs={{16,4},{18,6},{20,8},{22,10},{24,12},{26,14},{28,0},{30,2},{0,28},... | collective-permute-start | bytes 589832 | tf_op jit(solution)/shard_map/ppermute | solution.py:281
  66.9 5.9 %collective-permute-start.8 = (f32[1,384]{1,0:T(1,128)S(1)}, f32[1,384]{1,0:T(1,128)S(1)}, u32[]{:S(2)}, u32[]{:S(2)}) collective-permute-start(f32[1,384]{1,0:T(1,128)S(1)} %slice.13), channel_id=1, source_target_pairs={{0,28},{2,30},{4,16},{6,18},{8,20},{10,22},{12,24},{14,26},{1,29},... | collective-permute-start | bytes 4616 | tf_op jit(solution)/shard_map/ppermute | solution.py:281
  68.2 4.6 %collective-permute-start.7 = (f32[1,768]{1,0:T(1,128)S(1)}, f32[1,768]{1,0:T(1,128)S(1)}, u32[]{:S(2)}, u32[]{:S(2)}) collective-permute-start(f32[1,768]{1,0:T(1,128)S(1)} %slice.12), channel_id=1, source_target_pairs={{0,30},{2,16},{4,18},{6,20},{8,22},{10,24},{12,26},{14,28},{1,31},... | collective-permute-start | bytes 9224 | tf_op jit(solution)/shard_map/ppermute | solution.py:281
  72.9 10.2 %collective-permute-start.9 = (f32[384,512]{1,0:T(8,128)S(1)}, f32[384,512]{1,0:T(8,128)S(1)}, u32[]{:S(2)}, u32[]{:S(2)}) collective-permute-start(f32[384,512]{1,0:T(8,128)S(1)} %get-tuple-element.32), channel_id=1, source_target_pairs={{0,16},{2,18},{4,20},{6,22},{8,24},{10,26},{12,28},{14,30},{16,0},... | collective-permute-start | bytes 2359304 | tf_op jit(solution)/shard_map/ppermute | solution.py:281
  78.0 5.1 %collective-permute-start.11 = (f32[1,384]{1,0:T(1,128)S(1)}, f32[1,384]{1,0:T(1,128)S(1)}, u32[]{:S(2)}, u32[]{:S(2)}) collective-permute-start(f32[1,384]{1,0:T(1,128)S(1)} %get-tuple-element.36), channel_id=1, source_target_pairs={{0,1},{1,17},{2,3},{3,19},{4,5},{5,21},{6,7},{7,23},{8,9},{9,25},{... | collective-permute-start | bytes 4616 | tf_op jit(solution)/shard_map/ppermute | solution.py:277
  81.8 1.3 %collective-permute-start.10 = (f32[1,384]{1,0:T(1,128)S(1)}, f32[1,384]{1,0:T(1,128)S(1)}, u32[]{:S(2)}, u32[]{:S(2)}) collective-permute-start(f32[1,384]{1,0:T(1,128)S(1)} %get-tuple-element.37), channel_id=1, source_target_pairs={{0,0},{1,16},{2,2},{3,18},{4,4},{5,20},{6,6},{7,22},{8,8},{9,24},{... | collective-permute-start | bytes 4616 | tf_op jit(solution)/shard_map/ppermute | solution.py:277
where the time goes:
time: 118 us
  starting transfers between devices  49.8 us (42%)
  blocking collectives  33.1 us (28%)
  waiting for transfers between devices  25.7 us (22%)
  Pallas kernels  7.65 us (6%)
    all_to_all x1, blocking collectives, on_device(): lax.all_to_all(grad.reshape(peers, per_peer, features), WHERE, 0, 0, tile...  33.1 us
    ppermute x8, starting transfers between devices, along(): return lax.ppermute(value, ('c', 'y'), route)  24.5 us
    all_to_all x1, starting transfers between devices, on_device(): lax.all_to_all(embeddings.reshape(peers, per_peer, features), WHERE, 0, 0...  18.3 us
    ppermute x2, waiting for transfers between devices, fetch_order(): return lax.ppermute(order, ('c', 'zh'), [(c * 2 + h, c) for c in range(2)])  18.1 us
    pallas_call x8, Pallas kernels, call(): pl.pallas_call(kernel, out_shape=outputs, in_specs=[SMEM if a.ndim == 1 e...  7.65 us
    ppermute x8, waiting for transfers between devices, along(): return lax.ppermute(value, ('c', 'y'), route)  5.9 us
    ppermute x2, starting transfers between devices, send_loss(): return lax.ppermute(loss, ('c', 'zh'), [(z, z * 2 + h) for z in range(2)])  4.44 us
    ppermute x2, starting transfers between devices, fetch_order(): return lax.ppermute(order, ('c', 'zh'), [(c * 2 + h, c) for c in range(2)])  2.63 us
  transfers between devices with their start and end apart: 13, of which 5 were waited for; matrix products, arithmetic and copies ran while one was open for 0% of the time, Pallas kernels for 4%

commit v1 on v0

--- a/solution.py
+++ b/solution.py
@@ -77,11 +77,23 @@
             two_ref[...] = unit
 
 
-def near_kernel(core_ref, own_ref, sib_ref, n1_ref, n2_ref, e_ref, sums_ref):
+def relay_kernel(n1a_ref, n2a_ref, out_ref):
+    half = n1a_ref.shape[0]
+    out_ref[0:half] = n2a_ref[...]
+    out_ref[half:] = n1a_ref[...]
+
+
+def near_rows(n1a, n2a, n1b, n2b):
+    return jnp.concatenate([n2b[...], n1b[...], n2a[...], n1a[...]], axis=0)
+
+
+def near_kernel(
+    core_ref, own_ref, sib_ref, n1a_ref, n2a_ref, n1b_ref, n2b_ref, e_ref, sums_ref
+):
     core = core_ref[0]
     rows = own_ref.shape[0]
     chip = chip_rows(own_ref[...], sib_ref[...])
-    near = chip_rows(n2_ref[...], n1_ref[...])
+    near = near_rows(n1a_ref, n2a_ref, n1b_ref, n2b_ref)
     for b in range(2):
         e = jnp.exp(gamma * rows_by_rows(chip[b * rows : (b + 1) * rows], near))
         e_ref[b * rows : (b + 1) * rows] = e
@@ -113,13 +125,13 @@
 
 
 def far_kernel(
-    core_ref, own_ref, sib_ref, q1_ref, q2_ref, near_sums_ref, sums_ref, oa_ref, ob_ref,
-    f_ref, cols_ref, lanes_ref, loss_ref,
+    core_ref, own_ref, sib_ref, far_ref, near_sums_ref, sums_ref, oa_ref, ob_ref,
+    f_ref, cols_ref, lanes_ref, loss_ref, to_near_ref, to_far_ref,
 ):
     core = core_ref[0]
     rows = own_ref.shape[0]
     half = rows // 2
-    far = jnp.concatenate([q2_ref[...], q1_ref[...]], axis=0)
+    far = far_ref[...]
 
     @pl.when(core == 1)
     def _():
@@ -144,7 +156,11 @@
             on_pos = gamma * weight / pos_sum
             cols_ref[part, 0:1] = on_neg
             cols_ref[part, 1:2] = on_pos
-            lanes_ref[0:1, part] = as_row(on_neg)
+            row = as_row(on_neg)
+            lanes_ref[0:1, part] = row
+            to_near_ref[0:1, (1 - b) * rows : (2 - b) * rows] = row
+            if b == 0:
+                to_far_ref[...] = row
             lanes_ref[1:2, part] = as_row(on_pos)
             loss = jnp.log(1.0 + product)
             loss_ref[b : b + 1] = jnp.sum(
@@ -159,17 +175,18 @@
 
 
 def below_kernel(
-    core_ref, own_ref, sib_ref, n1_ref, n2_ref, q1_ref, q2_ref,
-    e_ref, d_ref, sign_ref, f_ref, cols_ref, lanes_ref, keep_ref, send_ref,
+    core_ref, own_ref, sib_ref, n1a_ref, n2a_ref, n1b_ref, n2b_ref, far_ref,
+    e_ref, d_ref, sign_ref, f_ref, cols_ref, lanes_ref, loss_ref, keep_ref, send_ref,
 ):
     core = core_ref[0]
 
     @pl.when(core == 0)
     def _():
         rows = own_ref.shape[0]
+        send_ref[rows : rows + 1, 0:rows] = loss_ref[1:2]
         chip = chip_rows(own_ref[...], sib_ref[...])
-        near = chip_rows(n2_ref[...], n1_ref[...])
-        far = jnp.concatenate([q2_ref[...], q1_ref[...]], axis=0)
+        near = near_rows(n1a_ref, n2a_ref, n1b_ref, n2b_ref)
+        far = far_ref[...]
         zero = jnp.zeros((1, rows), F32)
         for b in range(2):
             part = slice(b * rows, (b + 1) * rows)
@@ -204,16 +221,17 @@
 
 
 def above_kernel(
-    core_ref, n1_ref, n2_ref, q1_ref, q2_ref, e_ref, f_ref, on_near_ref, on_far_ref, keep_in, send_in,
+    core_ref, n1a_ref, n2a_ref, n1b_ref, n2b_ref, far_ref, e_ref, f_ref, on_near_ref, on_far_ref,
+    keep_in, send_in,
     keep_ref, send_ref,
 ):
     core = core_ref[0]
 
     @pl.when(core == 1)
     def _():
-        rows = n1_ref.shape[0]
-        near = chip_rows(n2_ref[...], n1_ref[...])
-        far = jnp.concatenate([q2_ref[...], q1_ref[...]], axis=0)
+        rows = far_ref.shape[0]
+        near = near_rows(n1a_ref, n2a_ref, n1b_ref, n2b_ref)
+        far = far_ref[...]
         for b in range(2):
             part = slice(b * rows, (b + 1) * rows)
             total = jnp.dot(
@@ -226,8 +244,11 @@
             split_store(b, total, keep_ref, send_ref)
 
 
-def final_kernel(x_ref, keep_ref, other_ref, la_ref, lb_ref, grad_ref, loss_ref):
-    loss_ref[...] = la_ref[...] + lb_ref[...]
+def final_kernel(core_ref, x_ref, keep_ref, other_ref, losses_ref, grad_ref, loss_ref):
+    rows = keep_ref.shape[0]
+    loss_ref[...] = jnp.where(
+        core_ref[0] == 0, losses_ref[0:1], other_ref[rows : rows + 1, 0:rows]
+    )
     features = x_ref.shape[-1]
     half = keep_ref.shape[0] // 2
     for which in range(2):
@@ -273,9 +294,6 @@
     def fetch_order(h):
         return lax.ppermute(order, ("c", "zh"), [(c * 2 + h, c) for c in range(2)])
 
-    def send_loss(loss, h):
-        return lax.ppermute(loss, ("c", "zh"), [(z, z * 2 + h) for z in range(2)])
-
     def along(value, moves):
         route = [(a * ring + y, b * ring + (y + s) % ring) for a, b, s in moves for y in range(ring)]
         return lax.ppermute(value, ("c", "y"), route)
@@ -290,44 +308,61 @@
     own, one, two = call(
         pack_kernel, (core, arrived, oa, ob), (block, half_block, half_block), 0.01
     )
-    n1 = along(own, ((0, 0, 1), (1, 1, -1)))
-    n2 = along(own, ((1, 0, 1), (0, 1, -1)))
-    q1 = along(one, ((0, 0, 2), (1, 1, -2)))
-    q2 = along(two, ((1, 0, 2), (0, 1, -2)))
+    straight = ((0, 0, 1), (1, 1, -1))
+    across = ((1, 0, 1), (0, 1, -1))
+    n1a = along(one, straight)
+    n2a = along(two, across)
+    n1b = along(two, straight)
+    n2b = along(one, across)
+    near = (n1a, n2a, n1b, n2b)
+    far = along(call(relay_kernel, (n1a, n2a), block, 0.01), straight)
     sib = along(own, ((0, 1, 0), (1, 0, 0)))
 
     sign = call(mask_kernel, (core, oa, ob), shape(2 * rows, 2 * rows), 0.5)
     e, near_sums = call(
-        near_kernel, (core, own, sib, n1, n2), (shape(2 * rows, 2 * rows), shape(2 * rows, 8)), 0.8
+        near_kernel, (core, own, sib, *near), (shape(2 * rows, 2 * rows), shape(2 * rows, 8)), 0.8
     )
     d, own_sums = call(
         own_kernel, (core, own, sib, sign), (shape(2 * rows, 2 * rows), shape(2 * rows, 8)), 0.8
     )
-    f, cols, lanes, loss = call(
+    f, cols, lanes, losses, to_near, to_far = call(
         far_kernel,
-        (core, own, sib, q1, q2, near_sums, own_sums, oa, ob),
-        (shape(rows, rows), shape(2 * rows, 8), shape(2, 2 * rows), shape(2, rows)),
+        (core, own, sib, far, near_sums, own_sums, oa, ob),
+        (
+            shape(rows, rows),
+            shape(2 * rows, 8),
+            shape(2, 2 * rows),
+            shape(2, rows),
+            shape(1, 2 * rows),
+            shape(1, rows),
+        ),
         0.2,
     )
-    on_near = along(lanes[0:1], ((0, 1, -1),))
-    on_far = along(lanes[0:1, 0:rows], ((0, 1, -2),))
-    half_grads = (shape(rows, features), shape(rows, features))
+    on_near = along(to_near, ((0, 1, -1),))
+    on_far = along(to_far, ((0, 1, -2),))
+    half_grads = (shape(rows, features), shape(rows + 8, features))
     keep, send = call(
-        below_kernel, (core, own, sib, n1, n2, q1, q2, e, d, sign, f, cols, lanes), half_grads, 1.4
+        below_kernel,
+        (core, own, sib, *near, far, e, d, sign, f, cols, lanes, losses),
+        half_grads,
+        1.4,
     )
     keep, send = call(
         above_kernel,
-        (core, n1, n2, q1, q2, e, f, on_near, on_far, keep, send),
+        (core, *near, far, e, f, on_near, on_far, keep, send),
         half_grads,
         0.8,
-        {9: 0, 10: 1},
+        {10: 0, 11: 1},
     )
     other = along(send, ((0, 1, 0), (1, 0, 0)))
-    grad, row_loss = call(
+    grad, loss = call(
         final_kernel,
-        (arrived, keep, other, send_loss(loss[0:1], 0), send_loss(loss[1:2], 1)),
+        (core, arrived, keep, other, losses),
         (shape(peers // 2, 2, per_peer, features, dtype=BF16), shape(1, rows)),
         0.01,
+    )
+    row_loss = lax.ppermute(
+        loss, ("c", "zh"), [(c * 2 + h, h * 2 + c) for h in range(2) for c in range(2)]
     )
     sent_back = lax.all_to_all(
         grad.reshape(peers, per_peer, features), WHERE, 0, 0, tiled=True

time: 118 us -> 113 us (0.958)
  the two profiles are of different devices: /device:TPU:56 before, /device:TPU:16 now
where the time goes in v1:
time: 113 us; the launch traced here: 112 us
  starting transfers between devices  55.9 us (49%)
  waiting for transfers between devices  46.2 us (41%)
  Pallas kernels  7.98 us (7%)
  local copies, waits for them, and re-layouts  1.31 us (1%)
    ppermute x9, starting transfers between devices, along(): return lax.ppermute(value, ('c', 'y'), route)  29.4 us
    all_to_all x1, waiting for transfers between devices, on_device(): lax.all_to_all(grad.reshape(peers, per_peer, features), WHERE, 0, 0, tile...  21.7 us
    all_to_all x1, starting transfers between devices, on_device(): lax.all_to_all(embeddings.reshape(peers, per_peer, features), WHERE, 0, 0...  18.3 us
    ppermute x2, waiting for transfers between devices, fetch_order(): return lax.ppermute(order, ('c', 'zh'), [(c * 2 + h, c) for c in range(2)])  18 us
    pallas_call x9, Pallas kernels, call(): pl.pallas_call(kernel, out_shape=outputs, in_specs=[SMEM if a.ndim == 1 e...  7.98 us
    ppermute x9, waiting for transfers between devices, along(): return lax.ppermute(value, ('c', 'y'), route)  5.32 us
    all_to_all x1, starting transfers between devices, on_device(): lax.all_to_all(grad.reshape(peers, per_peer, features), WHERE, 0, 0, tile...  4.93 us
    ppermute x2, starting transfers between devices, fetch_order(): return lax.ppermute(order, ('c', 'zh'), [(c * 2 + h, c) for c in range(2)])  2.62 us
  transfers between devices with their start and end apart: 14, of which 7 were waited for; matrix products, arithmetic and copies ran while one was open for 0% of the time, Pallas kernels for 5%

profile of v1, /device:TPU:16, one launch (start us, length us, event | category | flops | bytes accessed | tf_op | source)
XLA Modules:
  0.0 112.2 jit_solution(7563634517478495570)
XLA Ops:
  0.6 18.3 %all-to-all-start = ((bf16[48,8,512]{2,1,0:T(8,128)(2,1)}), bf16[48,8,512]{2,1,0:T(8,128)(2,1)S(1)}, u32[]{:S(2)}, u32[]{:S(2)}) async-start(bf16[48,8,512]{2,1,0:T(8,128)(2,1)} %bitcast.8), calls=%async_computation | async-start | bytes 786432 | tf_op jit(solution)/shard_map/all_to_all | solution.py:302
  18.9 1.3 %collective-permute-start = (s32[1,384]{1,0:T(1,128)}, s32[1,384]{1,0:T(1,128)S(1)}, u32[]{:S(2)}, u32[]{:S(2)}) collective-permute-start(s32[1,384]{1,0:T(1,128)} %param.3), channel_id=1, source_target_pairs={{0,0},{16,1},{2,2},{18,3},{4,4},{20,5},{6,6},{22,7},{8,8},{24,9},{... | collective-permute-start | bytes 4616 | tf_op jit(solution)/shard_map/ppermute | solution.py:295
  20.3 1.3 %collective-permute-start.1 = (s32[1,384]{1,0:T(1,128)}, s32[1,384]{1,0:T(1,128)S(1)}, u32[]{:S(2)}, u32[]{:S(2)}) collective-permute-start(s32[1,384]{1,0:T(1,128)} %param.3), channel_id=1, source_target_pairs={{1,0},{17,1},{3,2},{19,3},{5,4},{21,5},{7,6},{23,7},{9,8},{25,9},{... | collective-permute-start | bytes 4616 | tf_op jit(solution)/shard_map/ppermute | solution.py:295
  21.6 0.0 collective-permute-done.oa_ref
  21.6 18.0 %collective-permute-done.1.ob_ref = s32[1,384]{1,0:T(1,128)S(1)} collective-permute-done((s32[1,384]{1,0:T(1,128)}, s32[1,384]{1,0:T(1,128)S(1)}, u32[]{:S(2)}, u32[]{:S(2)}) %collective-permute-start.1) | collective-permute-done | bytes 1568 | tf_op jit(solution)/shard_map/ppermute | solution.py:295
  39.6 1.1 all-to-all-done
  40.7 0.3 shard_map.41
  41.0 3.5 %collective-permute-start.2 = (bf16[192,512]{1,0:T(8,128)(2,1)S(1)}, bf16[192,512]{1,0:T(8,128)(2,1)S(1)}, u32[]{:S(2)}, u32[]{:S(2)}) collective-permute-start(bf16[192,512]{1,0:T(8,128)(2,1)S(1)} %get-tuple-element.21), channel_id=1, source_target_pairs={{0,2},{2,4},{4,6},{6,8},{8,10},{10,12},{12,14},{14,0},{16,30},{18,... | collective-permute-start | bytes 589832 | tf_op jit(solution)/shard_map/ppermute | solution.py:299
  44.5 1.9 %collective-permute-start.3 = (bf16[192,512]{1,0:T(8,128)(2,1)S(1)}, bf16[192,512]{1,0:T(8,128)(2,1)S(1)}, u32[]{:S(2)}, u32[]{:S(2)}) collective-permute-start(bf16[192,512]{1,0:T(8,128)(2,1)S(1)} %get-tuple-element.22), channel_id=1, source_target_pairs={{16,2},{18,4},{20,6},{22,8},{24,10},{26,12},{28,14},{30,0},{0,30},... | collective-permute-start | bytes 589832 | tf_op jit(solution)/shard_map/ppermute | solution.py:299
  46.4 4.8 %collective-permute-start.7 = (bf16[384,512]{1,0:T(8,128)(2,1)S(1)}, bf16[384,512]{1,0:T(8,128)(2,1)S(1)}, u32[]{:S(2)}, u32[]{:S(2)}) collective-permute-start(bf16[384,512]{1,0:T(8,128)(2,1)S(1)} %get-tuple-element.23.own_ref), channel_id=1, source_target_pairs={{0,16},{2,18},{4,20},{6,22},{8,24},{10,26},{12,28},{14,30},{16,0},... | collective-permute-start | bytes 1179656 | tf_op jit(solution)/shard_map/ppermute | solution.py:299
  51.2 0.2 collective-permute-done.3.n2a_ref
  51.5 4.7 %collective-permute-start.6 = (bf16[384,512]{1,0:T(8,128)(2,1)S(1)}, bf16[384,512]{1,0:T(8,128)(2,1)S(1)}, u32[]{:S(2)}, u32[]{:S(2)}) collective-permute-start(bf16[384,512]{1,0:T(8,128)(2,1)S(1)} %shard_map.42), channel_id=1, source_target_pairs={{0,2},{2,4},{4,6},{6,8},{8,10},{10,12},{12,14},{14,0},{16,30},{18,... | collective-permute-start | bytes 1179656 | tf_op jit(solution)/shard_map/ppermute | solution.py:299
  56.2 3.9 %collective-permute-start.4 = (bf16[192,512]{1,0:T(8,128)(2,1)S(1)}, bf16[192,512]{1,0:T(8,128)(2,1)S(1)}, u32[]{:S(2)}, u32[]{:S(2)}) collective-permute-start(bf16[192,512]{1,0:T(8,128)(2,1)S(1)} %get-tuple-element.22), channel_id=1, source_target_pairs={{0,2},{2,4},{4,6},{6,8},{8,10},{10,12},{12,14},{14,0},{16,30},{18,... | collective-permute-start | bytes 589832 | tf_op jit(solution)/shard_map/ppermute | solution.py:299
  60.1 1.9 %collective-permute-start.5 = (bf16[192,512]{1,0:T(8,128)(2,1)S(1)}, bf16[192,512]{1,0:T(8,128)(2,1)S(1)}, u32[]{:S(2)}, u32[]{:S(2)}) collective-permute-start(bf16[192,512]{1,0:T(8,128)(2,1)S(1)} %get-tuple-element.21), channel_id=1, source_target_pairs={{16,2},{18,4},{20,6},{22,8},{24,10},{26,12},{28,14},{30,0},{0,30},... | collective-permute-start | bytes 589832 | tf_op jit(solution)/shard_map/ppermute | solution.py:299
  62.0 0.7 shard_map.44.sign_ref
  62.8 0.0 collective-permute-done.7.sib_ref
  62.8 1.2 %shard_map.45 = (f32[768,768]{1,0:T(8,128)S(1)}, f32[768,8]{1,0:T(8,128)S(1)}) custom-call(s32[1]{0:T(128)} %bitcast.core_ref, bf16[384,512]{1,0:T(8,128)(2,1)S(1)} %get-tuple-element.23.own_ref, bf16[384,512]{1,0:T(8,128)(2,1)S(1)} %collective-permute-done.7.sib_ref, f32[768,768]{1,0:T(8,128)S(1)} %shard_map.44.sign_ref), custom_call_target="tpu_custom_call" | custom-call | flops 800000000 | bytes 100000 | tf_op jit(solution)/shard_map/pallas_call | solution.py:273
  63.9 0.7 collective-permute-done.4.n1b_ref
  64.7 2.4 %collective-permute-done.5.n2b_ref = bf16[192,512]{1,0:T(8,128)(2,1)S(1)} collective-permute-done((bf16[192,512]{1,0:T(8,128)(2,1)S(1)}, bf16[192,512]{1,0:T(8,128)(2,1)S(1)}, u32[]{:S(2)}, u32[]{:S(2)}) %collective-permute-start.5) | collective-permute-done | bytes 196640 | tf_op jit(solution)/shard_map/ppermute | solution.py:299
  67.1 1.5 %shard_map.43 = (f32[768,768]{1,0:T(8,128)S(1)}, f32[768,8]{1,0:T(8,128)S(1)}) custom-call(s32[1]{0:T(128)} %bitcast.core_ref, bf16[384,512]{1,0:T(8,128)(2,1)S(1)} %get-tuple-element.23.own_ref, bf16[384,512]{1,0:T(8,128)(2,1)S(1)} %collective-permute-done.7.sib_ref, bf16[192,512]{1,0:T(8,128)(2,1)S(1)} %collective-permute-done.2.n1a_ref, ...), custom_call_target="tpu_custom_call" | custom-call | flops 800000000 | bytes 100000 | tf_op jit(solution)/shard_map/pallas_call | solution.py:273
  68.6 1.4 %shard_map.46 = (f32[384,384]{1,0:T(8,128)S(1)}, f32[768,8]{1,0:T(8,128)S(1)}, f32[2,768]{1,0:T(2,128)S(1)}, f32[2,384]{1,0:T(2,128)S(1)}, f32[1,768]{1,0:T(1,128)S(1)}, /*index=5*/f32[1,384]{1,0:T(1,128)S(1)}) custom-call(s32[1]{0:T(128)} %bitcast.core_ref, bf16[384,512]{1,0:T(8,128)(2,1)S(1)} %get-tuple-element.23.own_ref, ...), custom_call_target="tpu_custom_call" | custom-call | flops 200000000 | bytes 100000 | tf_op jit(solution)/shard_map/pallas_call | solution.py:273
  70.0 1.3 %collective-permute-start.8 = (f32[1,768]{1,0:T(1,128)S(1)}, f32[1,768]{1,0:T(1,128)S(1)}, u32[]{:S(2)}, u32[]{:S(2)}) collective-permute-start(f32[1,768]{1,0:T(1,128)S(1)} %get-tuple-element.28), channel_id=1, source_target_pairs={{0,30},{2,16},{4,18},{6,20},{8,22},{10,24},{12,26},{14,28},{1,31},... | collective-permute-start | bytes 9224 | tf_op jit(solution)/shard_map/ppermute | solution.py:299
  71.3 1.3 %collective-permute-start.9 = (f32[1,384]{1,0:T(1,128)S(1)}, f32[1,384]{1,0:T(1,128)S(1)}, u32[]{:S(2)}, u32[]{:S(2)}) collective-permute-start(f32[1,384]{1,0:T(1,128)S(1)} %get-tuple-element.29), channel_id=1, source_target_pairs={{0,28},{2,30},{4,16},{6,18},{8,20},{10,22},{12,24},{14,26},{1,29},... | collective-permute-start | bytes 4616 | tf_op jit(solution)/shard_map/ppermute | solution.py:299
  72.6 1.8 %shard_map.47 = (f32[384,512]{1,0:T(8,128)S(1)}, f32[392,512]{1,0:T(8,128)S(1)}) custom-call(s32[1]{0:T(128)} %bitcast.core_ref, bf16[384,512]{1,0:T(8,128)(2,1)S(1)} %get-tuple-element.23.own_ref, bf16[384,512]{1,0:T(8,128)(2,1)S(1)} %collective-permute-done.7.sib_ref, bf16[192,512]{1,0:T(8,128)(2,1)S(1)} %collective-permute-done.2.n1a_ref, ...), custom_call_target="tpu_custom_call" | custom-call | flops 1400000000 | bytes 100000 | tf_op jit(solution)/shard_map/pallas_call | solution.py:273
  74.5 6.1 %collective-permute-start.10 = (f32[392,512]{1,0:T(8,128)S(1)}, f32[392,512]{1,0:T(8,128)S(1)}, u32[]{:S(2)}, u32[]{:S(2)}) collective-permute-start(f32[392,512]{1,0:T(8,128)S(1)} %get-tuple-element.37), channel_id=1, source_target_pairs={{0,16},{2,18},{4,20},{6,22},{8,24},{10,26},{12,28},{14,30},{16,0},... | collective-permute-start | bytes 2408456 | tf_op jit(solution)/shard_map/ppermute | solution.py:299
  80.6 1.9 %collective-permute-done.10.other_ref = f32[392,512]{1,0:T(8,128)S(1)} collective-permute-done((f32[392,512]{1,0:T(8,128)S(1)}, f32[392,512]{1,0:T(8,128)S(1)}, u32[]{:S(2)}, u32[]{:S(2)}) %collective-permute-start.10) | collective-permute-done | bytes 802848 | tf_op jit(solution)/shard_map/ppermute | solution.py:299
  82.5 1.1 shard_map.49
  83.6 4.9 %all-to-all-start.1 = ((bf16[48,8,512]{2,1,0:T(8,128)(2,1)}), bf16[48,8,512]{2,1,0:T(8,128)(2,1)S(1)}, u32[]{:S(2)}, u32[]{:S(2)}) async-start(bf16[48,8,512]{2,1,0:T(8,128)(2,1)} %bitcast.3), calls=%async_computation.1 | async-start | bytes 786432 | tf_op jit(solution)/shard_map/all_to_all | solution.py:367
  88.5 0.7 collective-permute-start.11
  89.2 21.7 %all-to-all-done.1 = bf16[48,8,512]{2,1,0:T(8,128)(2,1)S(1)} async-done(((bf16[48,8,512]{2,1,0:T(8,128)(2,1)}), bf16[48,8,512]{2,1,0:T(8,128)(2,1)S(1)}, u32[]{:S(2)}, u32[]{:S(2)}) %all-to-all-start.1) | async-done | bytes 393248 | tf_op jit(solution)/shard_map/all_to_all | solution.py:367
  110.9 0.7 copy.10
  111.7 0.6 copy.11
  (7 shorter events, 0.1 us)
Async XLA Ops:
  0.6 40.1 %all-to-all-start = ((bf16[48,8,512]{2,1,0:T(8,128)(2,1)}), bf16[48,8,512]{2,1,0:T(8,128)(2,1)S(1)}, u32[]{:S(2)}, u32[]{:S(2)}) async-start(bf16[48,8,512]{2,1,0:T(8,128)(2,1)} %bitcast.8), calls=%async_computation | async-start | bytes 786432 | tf_op jit(solution)/shard_map/all_to_all | solution.py:302
  18.9 2.6 %collective-permute-start = (s32[1,384]{1,0:T(1,128)}, s32[1,384]{1,0:T(1,128)S(1)}, u32[]{:S(2)}, u32[]{:S(2)}) collective-permute-start(s32[1,384]{1,0:T(1,128)} %param.3), channel_id=1, source_target_pairs={{0,0},{16,1},{2,2},{18,3},{4,4},{20,5},{6,6},{22,7},{8,8},{24,9},{... | collective-permute-start | bytes 4616 | tf_op jit(solution)/shard_map/ppermute | solution.py:295
  20.3 19.3 %collective-permute-start.1 = (s32[1,384]{1,0:T(1,128)}, s32[1,384]{1,0:T(1,128)S(1)}, u32[]{:S(2)}, u32[]{:S(2)}) collective-permute-start(s32[1,384]{1,0:T(1,128)} %param.3), channel_id=1, source_target_pairs={{1,0},{17,1},{3,2},{19,3},{5,4},{21,5},{7,6},{23,7},{9,8},{25,9},{... | collective-permute-start | bytes 4616 | tf_op jit(solution)/shard_map/ppermute | solution.py:295
  41.0 10.2 %collective-permute-start.2 = (bf16[192,512]{1,0:T(8,128)(2,1)S(1)}, bf16[192,512]{1,0:T(8,128)(2,1)S(1)}, u32[]{:S(2)}, u32[]{:S(2)}) collective-permute-start(bf16[192,512]{1,0:T(8,128)(2,1)S(1)} %get-tuple-element.21), channel_id=1, source_target_pairs={{0,2},{2,4},{4,6},{6,8},{8,10},{10,12},{12,14},{14,0},{16,30},{18,... | collective-permute-start | bytes 589832 | tf_op jit(solution)/shard_map/ppermute | solution.py:299
  44.5 7.0 %collective-permute-start.3 = (bf16[192,512]{1,0:T(8,128)(2,1)S(1)}, bf16[192,512]{1,0:T(8,128)(2,1)S(1)}, u32[]{:S(2)}, u32[]{:S(2)}) collective-permute-start(bf16[192,512]{1,0:T(8,128)(2,1)S(1)} %get-tuple-element.22), channel_id=1, source_target_pairs={{16,2},{18,4},{20,6},{22,8},{24,10},{26,12},{28,14},{30,0},{0,30},... | collective-permute-start | bytes 589832 | tf_op jit(solution)/shard_map/ppermute | solution.py:299
  46.4 16.3 %collective-permute-start.7 = (bf16[384,512]{1,0:T(8,128)(2,1)S(1)}, bf16[384,512]{1,0:T(8,128)(2,1)S(1)}, u32[]{:S(2)}, u32[]{:S(2)}) collective-permute-start(bf16[384,512]{1,0:T(8,128)(2,1)S(1)} %get-tuple-element.23.own_ref), channel_id=1, source_target_pairs={{0,16},{2,18},{4,20},{6,22},{8,24},{10,26},{12,28},{14,30},{16,0},... | collective-permute-start | bytes 1179656 | tf_op jit(solution)/shard_map/ppermute | solution.py:299
  51.5 17.1 %collective-permute-start.6 = (bf16[384,512]{1,0:T(8,128)(2,1)S(1)}, bf16[384,512]{1,0:T(8,128)(2,1)S(1)}, u32[]{:S(2)}, u32[]{:S(2)}) collective-permute-start(bf16[384,512]{1,0:T(8,128)(2,1)S(1)} %shard_map.42), channel_id=1, source_target_pairs={{0,2},{2,4},{4,6},{6,8},{8,10},{10,12},{12,14},{14,0},{16,30},{18,... | collective-permute-start | bytes 1179656 | tf_op jit(solution)/shard_map/ppermute | solution.py:299
  56.2 8.4 %collective-permute-start.4 = (bf16[192,512]{1,0:T(8,128)(2,1)S(1)}, bf16[192,512]{1,0:T(8,128)(2,1)S(1)}, u32[]{:S(2)}, u32[]{:S(2)}) collective-permute-start(bf16[192,512]{1,0:T(8,128)(2,1)S(1)} %get-tuple-element.22), channel_id=1, source_target_pairs={{0,2},{2,4},{4,6},{6,8},{8,10},{10,12},{12,14},{14,0},{16,30},{18,... | collective-permute-start | bytes 589832 | tf_op jit(solution)/shard_map/ppermute | solution.py:299
  60.1 7.0 %collective-permute-start.5 = (bf16[192,512]{1,0:T(8,128)(2,1)S(1)}, bf16[192,512]{1,0:T(8,128)(2,1)S(1)}, u32[]{:S(2)}, u32[]{:S(2)}) collective-permute-start(bf16[192,512]{1,0:T(8,128)(2,1)S(1)} %get-tuple-element.21), channel_id=1, source_target_pairs={{16,2},{18,4},{20,6},{22,8},{24,10},{26,12},{28,14},{30,0},{0,30},... | collective-permute-start | bytes 589832 | tf_op jit(solution)/shard_map/ppermute | solution.py:299
  70.0 4.4 %collective-permute-start.8 = (f32[1,768]{1,0:T(1,128)S(1)}, f32[1,768]{1,0:T(1,128)S(1)}, u32[]{:S(2)}, u32[]{:S(2)}) collective-permute-start(f32[1,768]{1,0:T(1,128)S(1)} %get-tuple-element.28), channel_id=1, source_target_pairs={{0,30},{2,16},{4,18},{6,20},{8,22},{10,24},{12,26},{14,28},{1,31},... | collective-permute-start | bytes 9224 | tf_op jit(solution)/shard_map/ppermute | solution.py:299
  71.3 3.1 %collective-permute-start.9 = (f32[1,384]{1,0:T(1,128)S(1)}, f32[1,384]{1,0:T(1,128)S(1)}, u32[]{:S(2)}, u32[]{:S(2)}) collective-permute-start(f32[1,384]{1,0:T(1,128)S(1)} %get-tuple-element.29), channel_id=1, source_target_pairs={{0,28},{2,30},{4,16},{6,18},{8,20},{10,22},{12,24},{14,26},{1,29},... | collective-permute-start | bytes 4616 | tf_op jit(solution)/shard_map/ppermute | solution.py:299
  74.5 8.0 %collective-permute-start.10 = (f32[392,512]{1,0:T(8,128)S(1)}, f32[392,512]{1,0:T(8,128)S(1)}, u32[]{:S(2)}, u32[]{:S(2)}) collective-permute-start(f32[392,512]{1,0:T(8,128)S(1)} %get-tuple-element.37), channel_id=1, source_target_pairs={{0,16},{2,18},{4,20},{6,22},{8,24},{10,26},{12,28},{14,30},{16,0},... | collective-permute-start | bytes 2408456 | tf_op jit(solution)/shard_map/ppermute | solution.py:299
  83.6 27.3 %all-to-all-start.1 = ((bf16[48,8,512]{2,1,0:T(8,128)(2,1)}), bf16[48,8,512]{2,1,0:T(8,128)(2,1)S(1)}, u32[]{:S(2)}, u32[]{:S(2)}) async-start(bf16[48,8,512]{2,1,0:T(8,128)(2,1)} %bitcast.3), calls=%async_computation.1 | async-start | bytes 786432 | tf_op jit(solution)/shard_map/all_to_all | solution.py:367
  88.5 0.7 collective-permute-start.11

commit v2 on v1

v2 whole, which is shorter than its diff:
```python
import jax
import jax.numpy as jnp
from jax import lax
from jax.experimental import pallas as pl
from jax.experimental.pallas import tpu as pltpu
from jax.sharding import Mesh
from jax.sharding import PartitionSpec as P


K = 16
gamma = 16.0
F32 = jnp.float32
BF16 = jnp.bfloat16
WHERE = ("zl", "x", "zh")
LIMIT = 20 * 2**20


def rows_by_rows(a, b):
    return lax.dot_general(a, b, (((1,), (1,)), ((), ())), preferred_element_type=F32)


def chip_rows(own, sib):
    half = own.shape[0] // 2
    return jnp.concatenate([own[0:half], sib[0:half], own[half:], sib[half:]], axis=0)


def as_row(column):
    return jnp.broadcast_to(column, (column.shape[0], 128)).T[0:1]


def over_rows(value):
    return jnp.sum(value, axis=0, keepdims=True)


def over_columns(value):
    return jnp.sum(value, axis=1, keepdims=True)


def arrived_rows(order_ref):
    rows = order_ref.shape[1]
    half = rows // 2
    i = lax.broadcasted_iota(jnp.int32, (rows, rows), 0)
    source = jnp.where(i < half, 0, 1)
    i = i - source * half
    return (i // 8) * 16 + source * 8 + i % 8 == order_ref[...]


def classes_kernel(core_ref, o0_ref, o1_ref, o2_ref, sign_ref):
    core = core_ref[0]
    rows = o0_ref.shape[1]
    slot = lax.broadcasted_iota(jnp.int32, (rows, 128), 0) // K
    table = jnp.where(lax.broadcasted_iota(jnp.int32, (rows, 128), 1) == slot, 1.0, 0.0)
    table = table.astype(BF16)
    diagonal = lax.broadcasted_iota(jnp.int32, (rows, rows), 0) == lax.broadcasted_iota(
        jnp.int32, (rows, rows), 1
    )

    def fill(b, ref):
        chosen = jnp.where(arrived_rows(ref), 1.0, 0.0).astype(BF16)
        hot = jnp.dot(chosen, table, preferred_element_type=F32).astype(BF16)
        sign_ref[b] = jnp.where(diagonal, 0.0, 1.0 - 2.0 * rows_by_rows(hot, hot))

    fill(0, o0_ref)
    fill(1, o1_ref)

    @pl.when(core == 1)
    def _():
        fill(2, o2_ref)


def pack_kernel(core_ref, x_ref, o0_ref, o1_ref, o2_ref, full_ref, one_ref, two_ref):
    core = core_ref[0]
    half = one_ref.shape[0]
    for which in range(2):
        x = x_ref[:, which].astype(F32).reshape(half, x_ref.shape[-1])
        inv = lax.rsqrt(jnp.sum(x * x, axis=1, keepdims=True) + 1e-06)
        unit = (x * inv).astype(BF16)
        full_ref[which * half : (which + 1) * half] = unit

        @pl.when(core == 1 - which)
        def _():
            one_ref[...] = unit

        @pl.when(core == which)
        def _():
            two_ref[...] = unit


def relay_kernel(own_ref, n1a_ref, n2a_ref, out_ref, both_ref):
    half = n1a_ref.shape[0]
    rows = 2 * half
    out_ref[0:half] = n2a_ref[...]
    out_ref[half:] = n1a_ref[...]
    both_ref[0:rows] = own_ref[...]
    both_ref[rows : rows + half] = n2a_ref[...]
    both_ref[rows + half :] = n1a_ref[...]


def signed_exp(sign, sim):
    e = jnp.exp(gamma * sign * sim)
    return e, jnp.where(sign < 0.0, e, 0.0), jnp.where(sign > 0.0, e, 0.0)


def factors(pos_sum, neg_sum):
    product = pos_sum * neg_sum
    weight = product / (1.0 + product)
    return gamma * weight / neg_sum, gamma * weight / pos_sum, jnp.log(1.0 + product)


def early_kernel(
    core_ref, own_ref, both_ref, n1a_ref, n2a_ref, n1b_ref, n2b_ref, sign_ref,
    e_ref, d_ref, cols_ref, lanes_ref,
):
    core = core_ref[0]
    rows = own_ref.shape[0]
    chip = chip_rows(own_ref[...], both_ref[0:rows])
    b_part = (n2b_ref[...], n1b_ref[...])
    a_part = (n2a_ref[...], n1a_ref[...])
    near = jnp.concatenate(b_part + a_part, axis=0)

    @pl.when(core == 0)
    def _():
        for b in range(2):
            part = slice(b * rows, (b + 1) * rows)
            e = jnp.exp(gamma * rows_by_rows(chip[part], near))
            e_ref[part] = e
            neg_sum = over_columns(e)
            for other in range(2):
                there = slice(other * rows, (other + 1) * rows)
                sim = rows_by_rows(chip[part], chip[there])
                if other == b:
                    d, pos, neg = signed_exp(sign_ref[b], sim)
                    neg_sum = neg_sum + over_columns(neg)
                    cols_ref[part, 0:1] = over_columns(pos)
                else:
                    d = jnp.exp(gamma * sim)
                    if b == 1:
                        neg_sum = neg_sum + over_columns(d)
                d_ref[part, there] = d
            cols_ref[part, 1:2] = neg_sum

    @pl.when(core == 1)
    def _():
        below = both_ref[rows:]
        for b in range(2):
            part = slice(b * rows, (b + 1) * rows)
            anchors = near[part]
            e = jnp.exp(gamma * rows_by_rows(chip, anchors))
            e_ref[:, part] = e
            _, pos, neg = signed_exp(sign_ref[b], rows_by_rows(anchors, anchors))
            third = near[rows:] if b == 0 else below
            lanes_ref[0:1, part] = over_rows(pos)
            lanes_ref[1:2, part] = (
                over_rows(e) + over_rows(neg) + over_rows(jnp.exp(gamma * rows_by_rows(third, anchors)))
            )


def late_kernel(
    core_ref, own_ref, both_ref, n1a_ref, n2a_ref, n1b_ref, n2b_ref, far_ref, sign_ref,
    e_ref, d_ref, cols_ref, lanes_ref, o0_ref, o1_ref, keep_ref, send_ref, loss_ref,
):
    core = core_ref[0]
    rows = own_ref.shape[0]
    chip = chip_rows(own_ref[...], both_ref[0:rows])
    near = jnp.concatenate([n2b_ref[...], n1b_ref[...], n2a_ref[...], n1a_ref[...]], axis=0)
    far = far_ref[...]

    @pl.when(core == 0)
    def _():
        f = jnp.exp(gamma * rows_by_rows(chip[0:rows], far))
        on_neg, on_pos, row_neg, row_pos = [], [], [], []
        for b, order_ref in enumerate((o0_ref, o1_ref)):
            part = slice(b * rows, (b + 1) * rows)
            neg_sum = cols_ref[part, 1:2]
            if b == 0:
                neg_sum = neg_sum + over_columns(f)
            up, down, loss = factors(cols_ref[part, 0:1], neg_sum)
            on_neg.append(up)
            on_pos.append(down)
            row_neg.append(as_row(up))
            row_pos.append(as_row(down))
            by_slot = over_rows(jnp.where(arrived_rows(order_ref), loss, 0.0))
            if b == 0:
                loss_ref[...] = by_slot
            else:
                send_ref[rows : rows + 1, 0:rows] = by_slot
        for b in range(2):
            part = slice(b * rows, (b + 1) * rows)
            total = jnp.dot(
                (on_neg[b] * e_ref[part]).astype(BF16), near, preferred_element_type=F32
            )
            for other in range(2):
                there = slice(other * rows, (other + 1) * rows)
                if other == b:
                    sign = sign_ref[b]
                    up = on_neg[b] + row_neg[b]
                    down = on_pos[b] + row_pos[b]
                    scale = jnp.where(sign > 0.0, up, jnp.where(sign < 0.0, -down, 0.0))
                elif b == 0:
                    scale = row_neg[1]
                else:
                    scale = on_neg[1]
                coef = (scale * d_ref[part, there]).astype(BF16)
                total = total + jnp.dot(coef, chip[there], preferred_element_type=F32)
            if b == 0:
                coef = (on_neg[0] * f).astype(BF16)
                total = total + jnp.dot(coef, far, preferred_element_type=F32)
            split_store(b, total, keep_ref, send_ref)

    @pl.when(core == 1)
    def _():
        f = jnp.exp(gamma * rows_by_rows(chip[rows:], far))
        _, pos, neg = signed_exp(sign_ref[2], rows_by_rows(far, far))
        others = jnp.exp(gamma * rows_by_rows(near, far))
        on_far, _, _ = factors(over_rows(pos), over_rows(f) + over_rows(neg) + over_rows(others))
        on_near, _, _ = factors(lanes_ref[0:1], lanes_ref[1:2])
        for b in range(2):
            part = slice(b * rows, (b + 1) * rows)
            coef = (on_near * e_ref[part]).astype(BF16)
            total = jnp.dot(coef, near, preferred_element_type=F32)
            if b == 1:
                coef = (on_far * f).astype(BF16)
                total = total + jnp.dot(coef, far, preferred_element_type=F32)
            split_store(b, total, keep_ref, send_ref)
        loss_ref[...] = jnp.zeros_like(loss_ref)


def split_store(b, total, keep_ref, send_ref):
    half = total.shape[0] // 2
    keep_ref[b * half : (b + 1) * half] = total[0:half]
    send_ref[b * half : (b + 1) * half] = total[half:]


def final_kernel(core_ref, x_ref, keep_ref, other_ref, losses_ref, grad_ref, loss_ref):
    rows = keep_ref.shape[0]
    loss_ref[...] = jnp.where(
        core_ref[0] == 0, losses_ref[...], other_ref[rows : rows + 1, 0:rows]
    )
    features = x_ref.shape[-1]
    half = keep_ref.shape[0] // 2
    for which in range(2):
        part = slice(which * half, (which + 1) * half)
        total = keep_ref[part] + other_ref[part]
        x = x_ref[:, which].astype(F32).reshape(half, features)
        inv = lax.rsqrt(jnp.sum(x * x, axis=1, keepdims=True) + 1e-06)
        u = x * inv
        grad = (total - u * jnp.sum(u * total, axis=1, keepdims=True)) * inv
        grad_ref[:, which] = grad.reshape(half // 8, 8, features).astype(BF16)


def copy_kernel(x_ref, out_ref):
    out_ref[...] = x_ref[...]


VMEM = pl.BlockSpec(memory_space=pltpu.VMEM)
SMEM = pl.BlockSpec(memory_space=pltpu.SMEM)


def shape(*size, dtype=F32):
    return jax.ShapeDtypeStruct(size, dtype)


def call(kernel, inputs, outputs, work, aliases=None):
    return pl.pallas_call(
        kernel,
        out_shape=outputs,
        in_specs=[SMEM if a.ndim == 1 else VMEM for a in inputs],
        out_specs=jax.tree.map(lambda _: VMEM, outputs),
        input_output_aliases=aliases or {},
        compiler_params=pltpu.CompilerParams(vmem_limit_bytes=LIMIT),
        cost_estimate=pl.CostEstimate(
            flops=int(work * 10**9), bytes_accessed=10**5, transcendentals=0
        ),
    )(*inputs)


def on_device(embeddings, order):
    rows, features = embeddings.shape
    peers = lax.axis_size(WHERE)
    per_peer = rows // peers
    half = rows // 2
    core = lax.axis_index("c").astype(jnp.int32).reshape(1)
    ring = lax.axis_size("y")

    def fetch_order(moves):
        route = [
            ((c * ring + y) * 2 + h, (core * ring + (y + s) % ring) * 2 + c)
            for h, core, s in moves
            for c in range(2)
            for y in range(ring)
        ]
        return lax.ppermute(order, ("c", "y", "zh"), route)

    def along(value, moves):
        route = [(a * ring + y, b * ring + (y + s) % ring) for a, b, s in moves for y in range(ring)]
        return lax.ppermute(value, ("c", "y"), route)

    o0 = fetch_order(((0, 0, 0), (1, 1, -1)))
    o1 = fetch_order(((1, 0, 0), (0, 1, -1)))
    o2 = fetch_order(((0, 1, -2),))
    arrived = lax.all_to_all(
        embeddings.reshape(peers, per_peer, features), WHERE, 0, 0, tiled=True
    ).reshape(peers // 2, 2, per_peer, features)
    block = shape(rows, features, dtype=BF16)
    half_block = shape(half, features, dtype=BF16)

    own, one, two = call(
        pack_kernel, (core, arrived, o0, o1, o2), (block, half_block, half_block), 0.01
    )
    straight = ((0, 0, 1), (1, 1, -1))
    across = ((1, 0, 1), (0, 1, -1))
    n1a = along(one, straight)
    n2a = along(two, across)
    n1b = along(two, straight)
    n2b = along(one, across)
    near = (n1a, n2a, n1b, n2b)
    relay, both = call(
        relay_kernel, (own, n1a, n2a), (block, shape(2 * rows, features, dtype=BF16)), 0.01
    )
    far = along(relay, straight)
    sib = along(both, ((0, 1, 0), (1, 0, 0)))

    sign = call(classes_kernel, (core, o0, o1, o2), shape(3, rows, rows), 0.5)
    e, d, cols, lanes = call(
        early_kernel,
        (core, own, sib, *near, sign),
        (
            shape(2 * rows, 2 * rows),
            shape(2 * rows, 2 * rows),
            shape(2 * rows, 8),
            shape(8, 2 * rows),
        ),
        1.2,
    )
    keep, send, losses = call(
        late_kernel,
        (core, own, sib, *near, far, sign, e, d, cols, lanes, o0, o1),
        (shape(rows, features), shape(rows + 8, features), shape(1, rows)),
        1.4,
    )
    other = along(send, ((0, 1, 0), (1, 0, 0)))
    grad, loss = call(
        final_kernel,
        (core, arrived, keep, other, losses),
        (shape(peers // 2, 2, per_peer, features, dtype=BF16), shape(1, rows)),
        0.01,
    )
    row_loss = lax.ppermute(
        loss, ("c", "zh"), [(c * 2 + h, h * 2 + c) for h in range(2) for c in range(2)]
    )
    row_loss = call(copy_kernel, (row_loss,), shape(1, rows), 0.001)
    sent_back = lax.all_to_all(
        grad.reshape(peers, per_peer, features), WHERE, 0, 0, tiled=True
    )
    return sent_back.reshape(rows, features), row_loss


def solution(mesh):
    dp, grp = mesh.devices.shape
    parts = Mesh(
        mesh.devices.reshape(dp // 8, 4, 2, grp // 2, 2), ("zl", "x", "c", "y", "zh")
    )
    placed = P(("zl", "x", "c", "y", "zh"), None)

    def step(embeddings, order):
        return on_device(embeddings, order)

    step = jax.shard_map(
        step, mesh=parts, in_specs=(placed, placed), out_specs=(placed, placed), check_vma=False
    )
    return step
```

time: 113 us -> 115 us (1.018)
  the two profiles are of different devices: /device:TPU:16 before, /device:TPU:1 now
where the time goes in v2:
time: 115 us; the launch traced here: 114 us
  starting transfers between devices  81.2 us (71%)
  waiting for transfers between devices  24.1 us (21%)
  Pallas kernels  7.16 us (6%)
    ppermute x7, starting transfers between devices, along(): return lax.ppermute(value, ('c', 'y'), route)  28.9 us
    all_to_all x1, starting transfers between devices, on_device(): lax.all_to_all(embeddings.reshape(peers, per_peer, features), WHERE, 0, 0...  18.8 us
    ppermute x3, starting transfers between devices, fetch_order(): return lax.ppermute(order, ('c', 'y', 'zh'), route)  17.9 us
    ppermute x1, waiting for transfers between devices, on_device(): lax.ppermute(loss, ('c', 'zh'), [(c * 2 + h, h * 2 + c) for h in range(2)...  10.8 us
    ppermute x1, starting transfers between devices, on_device(): lax.ppermute(loss, ('c', 'zh'), [(c * 2 + h, h * 2 + c) for h in range(2)...  10.2 us
    ppermute x7, waiting for transfers between devices, along(): return lax.ppermute(value, ('c', 'y'), route)  9.02 us
    pallas_call x7, Pallas kernels, call(): pl.pallas_call(kernel, out_shape=outputs, in_specs=[SMEM if a.ndim == 1 e...  7.16 us
    all_to_all x1, starting transfers between devices, on_device(): lax.all_to_all(grad.reshape(peers, per_peer, features), WHERE, 0, 0, tile...  5.41 us
  transfers between devices with their start and end apart: 13, of which 6 were waited for; matrix products, arithmetic and copies ran while one was open for 0% of the time, Pallas kernels for 3%

profile of v2, /device:TPU:1, one launch (start us, length us, event | category | flops | bytes accessed | tf_op | source)
XLA Modules:
  0.0 114.0 jit_solution(10776150288599518855)
XLA Ops:
  0.6 18.8 %all-to-all-start = ((bf16[48,8,512]{2,1,0:T(8,128)(2,1)}), bf16[48,8,512]{2,1,0:T(8,128)(2,1)S(1)}, u32[]{:S(2)}, u32[]{:S(2)}) async-start(bf16[48,8,512]{2,1,0:T(8,128)(2,1)} %bitcast.8), calls=%async_computation | async-start | bytes 786432 | tf_op jit(solution)/shard_map/all_to_all | solution.py:301
  19.5 10.5 %collective-permute-start = (s32[1,384]{1,0:T(1,128)}, s32[1,384]{1,0:T(1,128)S(1)}, u32[]{:S(2)}, u32[]{:S(2)}) collective-permute-start(s32[1,384]{1,0:T(1,128)} %param.3), channel_id=1, source_target_pairs={{0,0},{2,2},{4,4},{6,6},{8,8},{10,10},{12,12},{14,14},{16,1},{18,3... | collective-permute-start | bytes 4616 | tf_op jit(solution)/shard_map/ppermute | solution.py:292
  29.9 5.5 %collective-permute-start.2 = (s32[1,384]{1,0:T(1,128)}, s32[1,384]{1,0:T(1,128)S(1)}, u32[]{:S(2)}, u32[]{:S(2)}) collective-permute-start(s32[1,384]{1,0:T(1,128)} %param.3), channel_id=1, source_target_pairs={{0,28},{2,30},{4,16},{6,18},{8,20},{10,22},{12,24},{14,26},{16,29}... | collective-permute-start | bytes 4616 | tf_op jit(solution)/shard_map/ppermute | solution.py:292
  35.5 1.9 %collective-permute-start.1 = (s32[1,384]{1,0:T(1,128)}, s32[1,384]{1,0:T(1,128)S(1)}, u32[]{:S(2)}, u32[]{:S(2)}) collective-permute-start(s32[1,384]{1,0:T(1,128)} %param.3), channel_id=1, source_target_pairs={{1,0},{3,2},{5,4},{7,6},{9,8},{11,10},{13,12},{15,14},{17,1},{19,3... | collective-permute-start | bytes 4616 | tf_op jit(solution)/shard_map/ppermute | solution.py:292
  37.4 4.3 %collective-permute-done.o0_ref = s32[1,384]{1,0:T(1,128)S(1)} collective-permute-done((s32[1,384]{1,0:T(1,128)}, s32[1,384]{1,0:T(1,128)S(1)}, u32[]{:S(2)}, u32[]{:S(2)}) %collective-permute-start) | collective-permute-done | bytes 1568 | tf_op jit(solution)/shard_map/ppermute | solution.py:292
  41.8 0.0 collective-permute-done.2.o2_ref
  41.8 0.0 collective-permute-done.1.o1_ref
  41.8 0.0 all-to-all-done
  41.8 0.3 shard_map.41
  42.0 3.3 %collective-permute-start.3 = (bf16[192,512]{1,0:T(8,128)(2,1)S(1)}, bf16[192,512]{1,0:T(8,128)(2,1)S(1)}, u32[]{:S(2)}, u32[]{:S(2)}) collective-permute-start(bf16[192,512]{1,0:T(8,128)(2,1)S(1)} %get-tuple-element.17), channel_id=1, source_target_pairs={{0,2},{2,4},{4,6},{6,8},{8,10},{10,12},{12,14},{14,0},{16,30},{18,... | collective-permute-start | bytes 589832 | tf_op jit(solution)/shard_map/ppermute | solution.py:296
  45.4 7.2 %collective-permute-start.4 = (bf16[192,512]{1,0:T(8,128)(2,1)S(1)}, bf16[192,512]{1,0:T(8,128)(2,1)S(1)}, u32[]{:S(2)}, u32[]{:S(2)}) collective-permute-start(bf16[192,512]{1,0:T(8,128)(2,1)S(1)} %get-tuple-element.18), channel_id=1, source_target_pairs={{16,2},{18,4},{20,6},{22,8},{24,10},{26,12},{28,14},{30,0},{0,30},... | collective-permute-start | bytes 589832 | tf_op jit(solution)/shard_map/ppermute | solution.py:296
  52.6 0.0 collective-permute-done.3.n1a_ref
  52.6 3.6 %collective-permute-done.4.n2a_ref = bf16[192,512]{1,0:T(8,128)(2,1)S(1)} collective-permute-done((bf16[192,512]{1,0:T(8,128)(2,1)S(1)}, bf16[192,512]{1,0:T(8,128)(2,1)S(1)}, u32[]{:S(2)}, u32[]{:S(2)}) %collective-permute-start.4) | collective-permute-done | bytes 196640 | tf_op jit(solution)/shard_map/ppermute | solution.py:296
  56.3 0.1 shard_map.42
  56.3 5.0 %collective-permute-start.5 = (bf16[768,512]{1,0:T(8,128)(2,1)S(1)}, bf16[768,512]{1,0:T(8,128)(2,1)S(1)}, u32[]{:S(2)}, u32[]{:S(2)}) collective-permute-start(bf16[768,512]{1,0:T(8,128)(2,1)S(1)} %get-tuple-element.19), channel_id=1, source_target_pairs={{0,16},{2,18},{4,20},{6,22},{8,24},{10,26},{12,28},{14,30},{16,0},... | collective-permute-start | bytes 2359304 | tf_op jit(solution)/shard_map/ppermute | solution.py:296
  61.4 2.9 %collective-permute-start.8 = (bf16[384,512]{1,0:T(8,128)(2,1)S(1)}, bf16[384,512]{1,0:T(8,128)(2,1)S(1)}, u32[]{:S(2)}, u32[]{:S(2)}) collective-permute-start(bf16[384,512]{1,0:T(8,128)(2,1)S(1)} %get-tuple-element.20), channel_id=1, source_target_pairs={{0,2},{2,4},{4,6},{6,8},{8,10},{10,12},{12,14},{14,0},{16,30},{18,... | collective-permute-start | bytes 1179656 | tf_op jit(solution)/shard_map/ppermute | solution.py:296
  64.3 1.9 %collective-permute-start.7 = (bf16[192,512]{1,0:T(8,128)(2,1)S(1)}, bf16[192,512]{1,0:T(8,128)(2,1)S(1)}, u32[]{:S(2)}, u32[]{:S(2)}) collective-permute-start(bf16[192,512]{1,0:T(8,128)(2,1)S(1)} %get-tuple-element.17), channel_id=1, source_target_pairs={{16,2},{18,4},{20,6},{22,8},{24,10},{26,12},{28,14},{30,0},{0,30},... | collective-permute-start | bytes 589832 | tf_op jit(solution)/shard_map/ppermute | solution.py:296
  66.2 3.5 %collective-permute-start.6 = (bf16[192,512]{1,0:T(8,128)(2,1)S(1)}, bf16[192,512]{1,0:T(8,128)(2,1)S(1)}, u32[]{:S(2)}, u32[]{:S(2)}) collective-permute-start(bf16[192,512]{1,0:T(8,128)(2,1)S(1)} %get-tuple-element.18), channel_id=1, source_target_pairs={{0,2},{2,4},{4,6},{6,8},{8,10},{10,12},{12,14},{14,0},{16,30},{18,... | collective-permute-start | bytes 589832 | tf_op jit(solution)/shard_map/ppermute | solution.py:296
  69.7 1.2 %shard_map.43.sign_ref = f32[3,384,384]{2,1,0:T(8,128)S(1)} custom-call(s32[1]{0:T(128)} %bitcast.core_ref, s32[1,384]{1,0:T(1,128)S(1)} %collective-permute-done.o0_ref, s32[1,384]{1,0:T(1,128)S(1)} %collective-permute-done.1.o1_ref, s32[1,384]{1,0:T(1,128)S(1)} %collective-permute-done.2.o2_ref), custom_call_target="tpu_custom_call" | custom-call | flops 500000000 | bytes 100000 | tf_op jit(solution)/shard_map/pallas_call | solution.py:264
  70.9 2.7 %collective-permute-done.7.n2b_ref = bf16[192,512]{1,0:T(8,128)(2,1)S(1)} collective-permute-done((bf16[192,512]{1,0:T(8,128)(2,1)S(1)}, bf16[192,512]{1,0:T(8,128)(2,1)S(1)}, u32[]{:S(2)}, u32[]{:S(2)}) %collective-permute-start.7) | collective-permute-done | bytes 196640 | tf_op jit(solution)/shard_map/ppermute | solution.py:296
  73.7 0.7 collective-permute-done.6.n1b_ref
  74.4 0.0 collective-permute-done.5.both_ref
  74.4 2.0 %shard_map.44 = (f32[768,768]{1,0:T(8,128)S(1)}, f32[768,768]{1,0:T(8,128)S(1)}, f32[768,8]{1,0:T(8,128)S(1)}, f32[8,768]{1,0:T(8,128)S(1)}) custom-call(s32[1]{0:T(128)} %bitcast.core_ref, bf16[384,512]{1,0:T(8,128)(2,1)S(1)} %get-tuple-element.16.own_ref, bf16[768,512]{1,0:T(8,128)(2,1)S(1)} %collective-permute-done.5.both_ref, ...), custom_call_target="tpu_custom_call" | custom-call | flops 1200000000 | bytes 100000 | tf_op jit(solution)/shard_map/pallas_call | solution.py:264
  76.4 2.0 %shard_map.45 = (f32[384,512]{1,0:T(8,128)S(1)}, f32[392,512]{1,0:T(8,128)S(1)}, f32[1,384]{1,0:T(1,128)S(1)}) custom-call(s32[1]{0:T(128)} %bitcast.core_ref, bf16[384,512]{1,0:T(8,128)(2,1)S(1)} %get-tuple-element.16.own_ref, bf16[768,512]{1,0:T(8,128)(2,1)S(1)} %collective-permute-done.5.both_ref, bf16[192,512]{1,0:T(8,128)(2,1)S(1)} %collective-permute-done.3.n1a_ref, ...), custom_call_target="tpu_custom_call" | custom-call | flops 1400000000 | bytes 100000 | tf_op jit(solution)/shard_map/pallas_call | solution.py:264
  78.4 5.0 %collective-permute-start.9 = (f32[392,512]{1,0:T(8,128)S(1)}, f32[392,512]{1,0:T(8,128)S(1)}, u32[]{:S(2)}, u32[]{:S(2)}) collective-permute-start(f32[392,512]{1,0:T(8,128)S(1)} %get-tuple-element.26), channel_id=1, source_target_pairs={{0,16},{2,18},{4,20},{6,22},{8,24},{10,26},{12,28},{14,30},{16,0},... | collective-permute-start | bytes 2408456 | tf_op jit(solution)/shard_map/ppermute | solution.py:296
  83.4 1.9 %collective-permute-done.9.other_ref = f32[392,512]{1,0:T(8,128)S(1)} collective-permute-done((f32[392,512]{1,0:T(8,128)S(1)}, f32[392,512]{1,0:T(8,128)S(1)}, u32[]{:S(2)}, u32[]{:S(2)}) %collective-permute-start.9) | collective-permute-done | bytes 802848 | tf_op jit(solution)/shard_map/ppermute | solution.py:296
  85.3 1.1 shard_map.46
  86.4 5.4 %all-to-all-start.1 = ((bf16[48,8,512]{2,1,0:T(8,128)(2,1)}), bf16[48,8,512]{2,1,0:T(8,128)(2,1)S(1)}, u32[]{:S(2)}, u32[]{:S(2)}) async-start(bf16[48,8,512]{2,1,0:T(8,128)(2,1)} %bitcast.3), calls=%async_computation.1 | async-start | bytes 786432 | tf_op jit(solution)/shard_map/all_to_all | solution.py:352
  91.8 10.2 %collective-permute-start.10 = (f32[1,384]{1,0:T(1,128)S(1)}, f32[1,384]{1,0:T(1,128)S(1)}, u32[]{:S(2)}, u32[]{:S(2)}) collective-permute-start(f32[1,384]{1,0:T(1,128)S(1)} %get-tuple-element.29), channel_id=1, source_target_pairs={{0,0},{16,1},{1,16},{17,17},{2,2},{18,3},{3,18},{19,19},{4,4},{20,... | collective-permute-start | bytes 4616 | tf_op jit(solution)/shard_map/ppermute | solution.py:348
  102.0 10.8 %collective-permute-done.10.x_ref = f32[1,384]{1,0:T(1,128)S(1)} collective-permute-done((f32[1,384]{1,0:T(1,128)S(1)}, f32[1,384]{1,0:T(1,128)S(1)}, u32[]{:S(2)}, u32[]{:S(2)}) %collective-permute-start.10) | collective-permute-done | bytes 1568 | tf_op jit(solution)/shard_map/ppermute | solution.py:348
  112.7 0.6 shard_map.47
  113.3 0.7 copy.5
  (2 shorter events, 0.0 us)
Async XLA Ops:
  0.6 41.1 %all-to-all-start = ((bf16[48,8,512]{2,1,0:T(8,128)(2,1)}), bf16[48,8,512]{2,1,0:T(8,128)(2,1)S(1)}, u32[]{:S(2)}, u32[]{:S(2)}) async-start(bf16[48,8,512]{2,1,0:T(8,128)(2,1)} %bitcast.8), calls=%async_computation | async-start | bytes 786432 | tf_op jit(solution)/shard_map/all_to_all | solution.py:301
  19.5 22.3 %collective-permute-start = (s32[1,384]{1,0:T(1,128)}, s32[1,384]{1,0:T(1,128)S(1)}, u32[]{:S(2)}, u32[]{:S(2)}) collective-permute-start(s32[1,384]{1,0:T(1,128)} %param.3), channel_id=1, source_target_pairs={{0,0},{2,2},{4,4},{6,6},{8,8},{10,10},{12,12},{14,14},{16,1},{18,3... | collective-permute-start | bytes 4616 | tf_op jit(solution)/shard_map/ppermute | solution.py:292
  29.9 11.8 %collective-permute-start.2 = (s32[1,384]{1,0:T(1,128)}, s32[1,384]{1,0:T(1,128)S(1)}, u32[]{:S(2)}, u32[]{:S(2)}) collective-permute-start(s32[1,384]{1,0:T(1,128)} %param.3), channel_id=1, source_target_pairs={{0,28},{2,30},{4,16},{6,18},{8,20},{10,22},{12,24},{14,26},{16,29}... | collective-permute-start | bytes 4616 | tf_op jit(solution)/shard_map/ppermute | solution.py:292
  35.5 6.3 %collective-permute-start.1 = (s32[1,384]{1,0:T(1,128)}, s32[1,384]{1,0:T(1,128)S(1)}, u32[]{:S(2)}, u32[]{:S(2)}) collective-permute-start(s32[1,384]{1,0:T(1,128)} %param.3), channel_id=1, source_target_pairs={{1,0},{3,2},{5,4},{7,6},{9,8},{11,10},{13,12},{15,14},{17,1},{19,3... | collective-permute-start | bytes 4616 | tf_op jit(solution)/shard_map/ppermute | solution.py:292
  42.0 10.6 %collective-permute-start.3 = (bf16[192,512]{1,0:T(8,128)(2,1)S(1)}, bf16[192,512]{1,0:T(8,128)(2,1)S(1)}, u32[]{:S(2)}, u32[]{:S(2)}) collective-permute-start(bf16[192,512]{1,0:T(8,128)(2,1)S(1)} %get-tuple-element.17), channel_id=1, source_target_pairs={{0,2},{2,4},{4,6},{6,8},{8,10},{10,12},{12,14},{14,0},{16,30},{18,... | collective-permute-start | bytes 589832 | tf_op jit(solution)/shard_map/ppermute | solution.py:296
  45.4 10.9 %collective-permute-start.4 = (bf16[192,512]{1,0:T(8,128)(2,1)S(1)}, bf16[192,512]{1,0:T(8,128)(2,1)S(1)}, u32[]{:S(2)}, u32[]{:S(2)}) collective-permute-start(bf16[192,512]{1,0:T(8,128)(2,1)S(1)} %get-tuple-element.18), channel_id=1, source_target_pairs={{16,2},{18,4},{20,6},{22,8},{24,10},{26,12},{28,14},{30,0},{0,30},... | collective-permute-start | bytes 589832 | tf_op jit(solution)/shard_map/ppermute | solution.py:296
  56.3 18.1 %collective-permute-start.5 = (bf16[768,512]{1,0:T(8,128)(2,1)S(1)}, bf16[768,512]{1,0:T(8,128)(2,1)S(1)}, u32[]{:S(2)}, u32[]{:S(2)}) collective-permute-start(bf16[768,512]{1,0:T(8,128)(2,1)S(1)} %get-tuple-element.19), channel_id=1, source_target_pairs={{0,16},{2,18},{4,20},{6,22},{8,24},{10,26},{12,28},{14,30},{16,0},... | collective-permute-start | bytes 2359304 | tf_op jit(solution)/shard_map/ppermute | solution.py:296
  61.4 15.0 %collective-permute-start.8 = (bf16[384,512]{1,0:T(8,128)(2,1)S(1)}, bf16[384,512]{1,0:T(8,128)(2,1)S(1)}, u32[]{:S(2)}, u32[]{:S(2)}) collective-permute-start(bf16[384,512]{1,0:T(8,128)(2,1)S(1)} %get-tuple-element.20), channel_id=1, source_target_pairs={{0,2},{2,4},{4,6},{6,8},{8,10},{10,12},{12,14},{14,0},{16,30},{18,... | collective-permute-start | bytes 1179656 | tf_op jit(solution)/shard_map/ppermute | solution.py:296
  64.3 9.4 %collective-permute-start.7 = (bf16[192,512]{1,0:T(8,128)(2,1)S(1)}, bf16[192,512]{1,0:T(8,128)(2,1)S(1)}, u32[]{:S(2)}, u32[]{:S(2)}) collective-permute-start(bf16[192,512]{1,0:T(8,128)(2,1)S(1)} %get-tuple-element.17), channel_id=1, source_target_pairs={{16,2},{18,4},{20,6},{22,8},{24,10},{26,12},{28,14},{30,0},{0,30},... | collective-permute-start | bytes 589832 | tf_op jit(solution)/shard_map/ppermute | solution.py:296
  66.2 8.2 %collective-permute-start.6 = (bf16[192,512]{1,0:T(8,128)(2,1)S(1)}, bf16[192,512]{1,0:T(8,128)(2,1)S(1)}, u32[]{:S(2)}, u32[]{:S(2)}) collective-permute-start(bf16[192,512]{1,0:T(8,128)(2,1)S(1)} %get-tuple-element.18), channel_id=1, source_target_pairs={{0,2},{2,4},{4,6},{6,8},{8,10},{10,12},{12,14},{14,0},{16,30},{18,... | collective-permute-start | bytes 589832 | tf_op jit(solution)/shard_map/ppermute | solution.py:296
  78.4 6.9 %collective-permute-start.9 = (f32[392,512]{1,0:T(8,128)S(1)}, f32[392,512]{1,0:T(8,128)S(1)}, u32[]{:S(2)}, u32[]{:S(2)}) collective-permute-start(f32[392,512]{1,0:T(8,128)S(1)} %get-tuple-element.26), channel_id=1, source_target_pairs={{0,16},{2,18},{4,20},{6,22},{8,24},{10,26},{12,28},{14,30},{16,0},... | collective-permute-start | bytes 2408456 | tf_op jit(solution)/shard_map/ppermute | solution.py:296
  86.4 26.9 %all-to-all-start.1 = ((bf16[48,8,512]{2,1,0:T(8,128)(2,1)}), bf16[48,8,512]{2,1,0:T(8,128)(2,1)S(1)}, u32[]{:S(2)}, u32[]{:S(2)}) async-start(bf16[48,8,512]{2,1,0:T(8,128)(2,1)} %bitcast.3), calls=%async_computation.1 | async-start | bytes 786432 | tf_op jit(solution)/shard_map/all_to_all | solution.py:352
  91.8 20.9 %collective-permute-start.10 = (f32[1,384]{1,0:T(1,128)S(1)}, f32[1,384]{1,0:T(1,128)S(1)}, u32[]{:S(2)}, u32[]{:S(2)}) collective-permute-start(f32[1,384]{1,0:T(1,128)S(1)} %get-tuple-element.29), channel_id=1, source_target_pairs={{0,0},{16,1},{1,16},{17,17},{2,2},{18,3},{3,18},{19,19},{4,4},{20,... | collective-permute-start | bytes 4616 | tf_op jit(solution)/shard_map/ppermute | solution.py:348

commit v3 on v2

--- a/solution.py
+++ b/solution.py
@@ -68,7 +68,7 @@
         fill(2, o2_ref)
 
 
-def pack_kernel(core_ref, x_ref, o0_ref, o1_ref, o2_ref, full_ref, one_ref, two_ref):
+def pack_kernel(core_ref, x_ref, full_ref, one_ref, two_ref):
     core = core_ref[0]
     half = one_ref.shape[0]
     for which in range(2):
@@ -304,9 +304,7 @@
     block = shape(rows, features, dtype=BF16)
     half_block = shape(half, features, dtype=BF16)
 
-    own, one, two = call(
-        pack_kernel, (core, arrived, o0, o1, o2), (block, half_block, half_block), 0.01
-    )
+    own, one, two = call(pack_kernel, (core, arrived), (block, half_block, half_block), 0.01)
     straight = ((0, 0, 1), (1, 1, -1))
     across = ((1, 0, 1), (0, 1, -1))
     n1a = along(one, straight)

time: 115 us -> 139 us (1.21)
  the two profiles are of different devices: /device:TPU:1 before, /device:TPU:8 now
where the time goes in v3:
time: 139 us; the launch traced here: 138 us
  starting transfers between devices  67.3 us (48%)
  waiting for transfers between devices  61.4 us (44%)
  Pallas kernels  7.69 us (6%)
    all_to_all x1, waiting for transfers between devices, on_device(): lax.all_to_all(embeddings.reshape(peers, per_peer, features), WHERE, 0, 0...  21.8 us
    all_to_all x1, waiting for transfers between devices, on_device(): lax.all_to_all(grad.reshape(peers, per_peer, features), WHERE, 0, 0, tile...  21.1 us
    ppermute x7, starting transfers between devices, along(): return lax.ppermute(value, ('c', 'y'), route)  19.3 us
    ppermute x3, starting transfers between devices, fetch_order(): return lax.ppermute(order, ('c', 'y', 'zh'), route)  19.1 us
    all_to_all x1, starting transfers between devices, on_device(): lax.all_to_all(embeddings.reshape(peers, per_peer, features), WHERE, 0, 0...  18.3 us
    ppermute x3, waiting for transfers between devices, fetch_order(): return lax.ppermute(order, ('c', 'y', 'zh'), route)  11.2 us
    all_to_all x1, starting transfers between devices, on_device(): lax.all_to_all(grad.reshape(peers, per_peer, features), WHERE, 0, 0, tile...  9.81 us
    pallas_call x7, Pallas kernels, call(): pl.pallas_call(kernel, out_shape=outputs, in_specs=[SMEM if a.ndim == 1 e...  7.69 us
  transfers between devices with their start and end apart: 13, of which 7 were waited for; matrix products, arithmetic and copies ran while one was open for 0% of the time, Pallas kernels for 2%

profile of v3, /device:TPU:8, one launch (start us, length us, event | category | flops | bytes accessed | tf_op | source)
XLA Modules:
  0.0 138.0 jit_solution(756762864824146512)
XLA Ops:
  0.6 18.3 %all-to-all-start = ((bf16[48,8,512]{2,1,0:T(8,128)(2,1)}), bf16[48,8,512]{2,1,0:T(8,128)(2,1)S(1)}, u32[]{:S(2)}, u32[]{:S(2)}) async-start(bf16[48,8,512]{2,1,0:T(8,128)(2,1)} %bitcast.8), calls=%async_computation | async-start | bytes 786432 | tf_op jit(solution)/shard_map/all_to_all | solution.py:301
  18.9 21.8 %all-to-all-done = bf16[48,8,512]{2,1,0:T(8,128)(2,1)S(1)} async-done(((bf16[48,8,512]{2,1,0:T(8,128)(2,1)}), bf16[48,8,512]{2,1,0:T(8,128)(2,1)S(1)}, u32[]{:S(2)}, u32[]{:S(2)}) %all-to-all-start) | async-done | bytes 393248 | tf_op jit(solution)/shard_map/all_to_all | solution.py:301
  40.7 0.3 shard_map.41
  41.0 3.5 %collective-permute-start = (bf16[192,512]{1,0:T(8,128)(2,1)S(1)}, bf16[192,512]{1,0:T(8,128)(2,1)S(1)}, u32[]{:S(2)}, u32[]{:S(2)}) collective-permute-start(bf16[192,512]{1,0:T(8,128)(2,1)S(1)} %get-tuple-element.17), channel_id=1, source_target_pairs={{0,2},{2,4},{4,6},{6,8},{8,10},{10,12},{12,14},{14,0},{16,30},{18,... | collective-permute-start | bytes 589832 | tf_op jit(solution)/shard_map/ppermute | solution.py:296
  44.5 1.9 %collective-permute-start.1 = (bf16[192,512]{1,0:T(8,128)(2,1)S(1)}, bf16[192,512]{1,0:T(8,128)(2,1)S(1)}, u32[]{:S(2)}, u32[]{:S(2)}) collective-permute-start(bf16[192,512]{1,0:T(8,128)(2,1)S(1)} %get-tuple-element.18), channel_id=1, source_target_pairs={{16,2},{18,4},{20,6},{22,8},{24,10},{26,12},{28,14},{30,0},{0,30},... | collective-permute-start | bytes 589832 | tf_op jit(solution)/shard_map/ppermute | solution.py:296
  46.4 2.1 %collective-permute-done.n1a_ref = bf16[192,512]{1,0:T(8,128)(2,1)S(1)} collective-permute-done((bf16[192,512]{1,0:T(8,128)(2,1)S(1)}, bf16[192,512]{1,0:T(8,128)(2,1)S(1)}, u32[]{:S(2)}, u32[]{:S(2)}) %collective-permute-start) | collective-permute-done | bytes 196640 | tf_op jit(solution)/shard_map/ppermute | solution.py:296
  48.6 2.9 %collective-permute-done.1.n2a_ref = bf16[192,512]{1,0:T(8,128)(2,1)S(1)} collective-permute-done((bf16[192,512]{1,0:T(8,128)(2,1)S(1)}, bf16[192,512]{1,0:T(8,128)(2,1)S(1)}, u32[]{:S(2)}, u32[]{:S(2)}) %collective-permute-start.1) | collective-permute-done | bytes 196640 | tf_op jit(solution)/shard_map/ppermute | solution.py:296
  51.5 0.1 shard_map.42
  51.6 2.0 %collective-permute-start.2 = (bf16[768,512]{1,0:T(8,128)(2,1)S(1)}, bf16[768,512]{1,0:T(8,128)(2,1)S(1)}, u32[]{:S(2)}, u32[]{:S(2)}) collective-permute-start(bf16[768,512]{1,0:T(8,128)(2,1)S(1)} %get-tuple-element.19), channel_id=1, source_target_pairs={{0,16},{2,18},{4,20},{6,22},{8,24},{10,26},{12,28},{14,30},{16,0},... | collective-permute-start | bytes 2359304 | tf_op jit(solution)/shard_map/ppermute | solution.py:296
  53.6 4.5 %collective-permute-start.5 = (bf16[384,512]{1,0:T(8,128)(2,1)S(1)}, bf16[384,512]{1,0:T(8,128)(2,1)S(1)}, u32[]{:S(2)}, u32[]{:S(2)}) collective-permute-start(bf16[384,512]{1,0:T(8,128)(2,1)S(1)} %get-tuple-element.20), channel_id=1, source_target_pairs={{0,2},{2,4},{4,6},{6,8},{8,10},{10,12},{12,14},{14,0},{16,30},{18,... | collective-permute-start | bytes 1179656 | tf_op jit(solution)/shard_map/ppermute | solution.py:296
  58.1 2.1 %collective-permute-start.4 = (bf16[192,512]{1,0:T(8,128)(2,1)S(1)}, bf16[192,512]{1,0:T(8,128)(2,1)S(1)}, u32[]{:S(2)}, u32[]{:S(2)}) collective-permute-start(bf16[192,512]{1,0:T(8,128)(2,1)S(1)} %get-tuple-element.17), channel_id=1, source_target_pairs={{16,2},{18,4},{20,6},{22,8},{24,10},{26,12},{28,14},{30,0},{0,30},... | collective-permute-start | bytes 589832 | tf_op jit(solution)/shard_map/ppermute | solution.py:296
  60.2 3.4 %collective-permute-start.3 = (bf16[192,512]{1,0:T(8,128)(2,1)S(1)}, bf16[192,512]{1,0:T(8,128)(2,1)S(1)}, u32[]{:S(2)}, u32[]{:S(2)}) collective-permute-start(bf16[192,512]{1,0:T(8,128)(2,1)S(1)} %get-tuple-element.18), channel_id=1, source_target_pairs={{0,2},{2,4},{4,6},{6,8},{8,10},{10,12},{12,14},{14,0},{16,30},{18,... | collective-permute-start | bytes 589832 | tf_op jit(solution)/shard_map/ppermute | solution.py:296
  63.6 1.3 collective-permute-start.6
  64.9 0.0 collective-permute-done.6.o0_ref
  65.0 15.5 %collective-permute-start.8 = (s32[1,384]{1,0:T(1,128)}, s32[1,384]{1,0:T(1,128)S(1)}, u32[]{:S(2)}, u32[]{:S(2)}) collective-permute-start(s32[1,384]{1,0:T(1,128)} %param.3), channel_id=1, source_target_pairs={{0,28},{2,30},{4,16},{6,18},{8,20},{10,22},{12,24},{14,26},{16,29}... | collective-permute-start | bytes 4616 | tf_op jit(solution)/shard_map/ppermute | solution.py:292
  80.5 1.5 %collective-permute-done.8.o2_ref = s32[1,384]{1,0:T(1,128)S(1)} collective-permute-done((s32[1,384]{1,0:T(1,128)}, s32[1,384]{1,0:T(1,128)S(1)}, u32[]{:S(2)}, u32[]{:S(2)}) %collective-permute-start.8) | collective-permute-done | bytes 1568 | tf_op jit(solution)/shard_map/ppermute | solution.py:292
  82.0 2.3 %collective-permute-start.7 = (s32[1,384]{1,0:T(1,128)}, s32[1,384]{1,0:T(1,128)S(1)}, u32[]{:S(2)}, u32[]{:S(2)}) collective-permute-start(s32[1,384]{1,0:T(1,128)} %param.3), channel_id=1, source_target_pairs={{1,0},{3,2},{5,4},{7,6},{9,8},{11,10},{13,12},{15,14},{17,1},{19,3... | collective-permute-start | bytes 4616 | tf_op jit(solution)/shard_map/ppermute | solution.py:292
  84.3 9.7 %collective-permute-done.7.o1_ref = s32[1,384]{1,0:T(1,128)S(1)} collective-permute-done((s32[1,384]{1,0:T(1,128)}, s32[1,384]{1,0:T(1,128)S(1)}, u32[]{:S(2)}, u32[]{:S(2)}) %collective-permute-start.7) | collective-permute-done | bytes 1568 | tf_op jit(solution)/shard_map/ppermute | solution.py:292
  93.9 0.8 shard_map.43.sign_ref
  94.7 0.0 collective-permute-done.4.n2b_ref
  94.7 0.0 collective-permute-done.3.n1b_ref
  94.7 0.0 collective-permute-done.2.both_ref
  94.8 1.9 %shard_map.44 = (f32[768,768]{1,0:T(8,128)S(1)}, f32[768,768]{1,0:T(8,128)S(1)}, f32[768,8]{1,0:T(8,128)S(1)}, f32[8,768]{1,0:T(8,128)S(1)}) custom-call(s32[1]{0:T(128)} %bitcast.core_ref, bf16[384,512]{1,0:T(8,128)(2,1)S(1)} %get-tuple-element.16.own_ref, bf16[768,512]{1,0:T(8,128)(2,1)S(1)} %collective-permute-done.2.both_ref, ...), custom_call_target="tpu_custom_call" | custom-call | flops 1200000000 | bytes 100000 | tf_op jit(solution)/shard_map/pallas_call | solution.py:264
  96.7 3.0 %shard_map.45 = (f32[384,512]{1,0:T(8,128)S(1)}, f32[392,512]{1,0:T(8,128)S(1)}, f32[1,384]{1,0:T(1,128)S(1)}) custom-call(s32[1]{0:T(128)} %bitcast.core_ref, bf16[384,512]{1,0:T(8,128)(2,1)S(1)} %get-tuple-element.16.own_ref, bf16[768,512]{1,0:T(8,128)(2,1)S(1)} %collective-permute-done.2.both_ref, bf16[192,512]{1,0:T(8,128)(2,1)S(1)} %collective-permute-done.n1a_ref, ...), custom_call_target="tpu_custom_call" | custom-call | flops 1400000000 | bytes 100000 | tf_op jit(solution)/shard_map/pallas_call | solution.py:264
  99.7 1.9 %collective-permute-start.9 = (f32[392,512]{1,0:T(8,128)S(1)}, f32[392,512]{1,0:T(8,128)S(1)}, u32[]{:S(2)}, u32[]{:S(2)}) collective-permute-start(f32[392,512]{1,0:T(8,128)S(1)} %get-tuple-element.26), channel_id=1, source_target_pairs={{0,16},{2,18},{4,20},{6,22},{8,24},{10,26},{12,28},{14,30},{16,0},... | collective-permute-start | bytes 2408456 | tf_op jit(solution)/shard_map/ppermute | solution.py:296
  101.7 2.3 %collective-permute-done.9.other_ref = f32[392,512]{1,0:T(8,128)S(1)} collective-permute-done((f32[392,512]{1,0:T(8,128)S(1)}, f32[392,512]{1,0:T(8,128)S(1)}, u32[]{:S(2)}, u32[]{:S(2)}) %collective-permute-start.9) | collective-permute-done | bytes 802848 | tf_op jit(solution)/shard_map/ppermute | solution.py:296
  103.9 1.1 shard_map.46
  105.0 9.8 %all-to-all-start.1 = ((bf16[48,8,512]{2,1,0:T(8,128)(2,1)}), bf16[48,8,512]{2,1,0:T(8,128)(2,1)S(1)}, u32[]{:S(2)}, u32[]{:S(2)}) async-start(bf16[48,8,512]{2,1,0:T(8,128)(2,1)} %bitcast.3), calls=%async_computation.1 | async-start | bytes 786432 | tf_op jit(solution)/shard_map/all_to_all | solution.py:350
  114.8 0.7 collective-permute-start.10
  115.5 0.6 shard_map.47
  116.1 21.1 %all-to-all-done.1 = bf16[48,8,512]{2,1,0:T(8,128)(2,1)S(1)} async-done(((bf16[48,8,512]{2,1,0:T(8,128)(2,1)}), bf16[48,8,512]{2,1,0:T(8,128)(2,1)S(1)}, u32[]{:S(2)}, u32[]{:S(2)}) %all-to-all-start.1) | async-done | bytes 393248 | tf_op jit(solution)/shard_map/all_to_all | solution.py:350
  137.2 0.7 copy.5
  (2 shorter events, 0.0 us)
Async XLA Ops:
  0.6 40.1 %all-to-all-start = ((bf16[48,8,512]{2,1,0:T(8,128)(2,1)}), bf16[48,8,512]{2,1,0:T(8,128)(2,1)S(1)}, u32[]{:S(2)}, u32[]{:S(2)}) async-start(bf16[48,8,512]{2,1,0:T(8,128)(2,1)} %bitcast.8), calls=%async_computation | async-start | bytes 786432 | tf_op jit(solution)/shard_map/all_to_all | solution.py:301
  41.0 7.6 %collective-permute-start = (bf16[192,512]{1,0:T(8,128)(2,1)S(1)}, bf16[192,512]{1,0:T(8,128)(2,1)S(1)}, u32[]{:S(2)}, u32[]{:S(2)}) collective-permute-start(bf16[192,512]{1,0:T(8,128)(2,1)S(1)} %get-tuple-element.17), channel_id=1, source_target_pairs={{0,2},{2,4},{4,6},{6,8},{8,10},{10,12},{12,14},{14,0},{16,30},{18,... | collective-permute-start | bytes 589832 | tf_op jit(solution)/shard_map/ppermute | solution.py:296
  44.5 7.0 %collective-permute-start.1 = (bf16[192,512]{1,0:T(8,128)(2,1)S(1)}, bf16[192,512]{1,0:T(8,128)(2,1)S(1)}, u32[]{:S(2)}, u32[]{:S(2)}) collective-permute-start(bf16[192,512]{1,0:T(8,128)(2,1)S(1)} %get-tuple-element.18), channel_id=1, source_target_pairs={{16,2},{18,4},{20,6},{22,8},{24,10},{26,12},{28,14},{30,0},{0,30},... | collective-permute-start | bytes 589832 | tf_op jit(solution)/shard_map/ppermute | solution.py:296
  51.6 43.2 %collective-permute-start.2 = (bf16[768,512]{1,0:T(8,128)(2,1)S(1)}, bf16[768,512]{1,0:T(8,128)(2,1)S(1)}, u32[]{:S(2)}, u32[]{:S(2)}) collective-permute-start(bf16[768,512]{1,0:T(8,128)(2,1)S(1)} %get-tuple-element.19), channel_id=1, source_target_pairs={{0,16},{2,18},{4,20},{6,22},{8,24},{10,26},{12,28},{14,30},{16,0},... | collective-permute-start | bytes 2359304 | tf_op jit(solution)/shard_map/ppermute | solution.py:296
  53.6 43.1 %collective-permute-start.5 = (bf16[384,512]{1,0:T(8,128)(2,1)S(1)}, bf16[384,512]{1,0:T(8,128)(2,1)S(1)}, u32[]{:S(2)}, u32[]{:S(2)}) collective-permute-start(bf16[384,512]{1,0:T(8,128)(2,1)S(1)} %get-tuple-element.20), channel_id=1, source_target_pairs={{0,2},{2,4},{4,6},{6,8},{8,10},{10,12},{12,14},{14,0},{16,30},{18,... | collective-permute-start | bytes 1179656 | tf_op jit(solution)/shard_map/ppermute | solution.py:296
  58.1 36.6 %collective-permute-start.4 = (bf16[192,512]{1,0:T(8,128)(2,1)S(1)}, bf16[192,512]{1,0:T(8,128)(2,1)S(1)}, u32[]{:S(2)}, u32[]{:S(2)}) collective-permute-start(bf16[192,512]{1,0:T(8,128)(2,1)S(1)} %get-tuple-element.17), channel_id=1, source_target_pairs={{16,2},{18,4},{20,6},{22,8},{24,10},{26,12},{28,14},{30,0},{0,30},... | collective-permute-start | bytes 589832 | tf_op jit(solution)/shard_map/ppermute | solution.py:296
  60.2 34.5 %collective-permute-start.3 = (bf16[192,512]{1,0:T(8,128)(2,1)S(1)}, bf16[192,512]{1,0:T(8,128)(2,1)S(1)}, u32[]{:S(2)}, u32[]{:S(2)}) collective-permute-start(bf16[192,512]{1,0:T(8,128)(2,1)S(1)} %get-tuple-element.18), channel_id=1, source_target_pairs={{0,2},{2,4},{4,6},{6,8},{8,10},{10,12},{12,14},{14,0},{16,30},{18,... | collective-permute-start | bytes 589832 | tf_op jit(solution)/shard_map/ppermute | solution.py:296
  63.6 1.3 collective-permute-start.6
  65.0 17.0 %collective-permute-start.8 = (s32[1,384]{1,0:T(1,128)}, s32[1,384]{1,0:T(1,128)S(1)}, u32[]{:S(2)}, u32[]{:S(2)}) collective-permute-start(s32[1,384]{1,0:T(1,128)} %param.3), channel_id=1, source_target_pairs={{0,28},{2,30},{4,16},{6,18},{8,20},{10,22},{12,24},{14,26},{16,29}... | collective-permute-start | bytes 4616 | tf_op jit(solution)/shard_map/ppermute | solution.py:292
  82.0 12.0 %collective-permute-start.7 = (s32[1,384]{1,0:T(1,128)}, s32[1,384]{1,0:T(1,128)S(1)}, u32[]{:S(2)}, u32[]{:S(2)}) collective-permute-start(s32[1,384]{1,0:T(1,128)} %param.3), channel_id=1, source_target_pairs={{1,0},{3,2},{5,4},{7,6},{9,8},{11,10},{13,12},{15,14},{17,1},{19,3... | collective-permute-start | bytes 4616 | tf_op jit(solution)/shard_map/ppermute | solution.py:292
  99.7 4.2 %collective-permute-start.9 = (f32[392,512]{1,0:T(8,128)S(1)}, f32[392,512]{1,0:T(8,128)S(1)}, u32[]{:S(2)}, u32[]{:S(2)}) collective-permute-start(f32[392,512]{1,0:T(8,128)S(1)} %get-tuple-element.26), channel_id=1, source_target_pairs={{0,16},{2,18},{4,20},{6,22},{8,24},{10,26},{12,28},{14,30},{16,0},... | collective-permute-start | bytes 2408456 | tf_op jit(solution)/shard_map/ppermute | solution.py:296
  105.0 32.2 %all-to-all-start.1 = ((bf16[48,8,512]{2,1,0:T(8,128)(2,1)}), bf16[48,8,512]{2,1,0:T(8,128)(2,1)S(1)}, u32[]{:S(2)}, u32[]{:S(2)}) async-start(bf16[48,8,512]{2,1,0:T(8,128)(2,1)} %bitcast.3), calls=%async_computation.1 | async-start | bytes 786432 | tf_op jit(solution)/shard_map/all_to_all | solution.py:350
  114.8 0.7 collective-permute-start.10
